TPU v7x, 256 devices: a whole 4x4x8 slice. The times are simulated.
256 devices in a mesh: dp: 32 (over x, z_hi, y), col: 8 (over z_lo, core).
Axes of the slice: x: 4, y: 4, z: 8 (z_hi: 2, z_lo: 4; z = z_hi * 4 + z_lo), core: 2. Of those that a mesh axis runs over, the one named last changes fastest.
Arguments:
- embeddings: bfloat16 [16384, 4096], P('dp'), may hold values from -16 to 16
- rotation: bfloat16 [4096, 4096], P(None, 'col'), may hold values from -0.09375 to 0.09375
- codes: int32 [16384, 512], P('dp', 'col'), may hold values from 0 to 255
- codebooks: bfloat16 [512, 256, 8], P('col'), may hold values from -16 to 16
Outputs:
- new_rotation: float32 [4096, 4096], P('dp', 'col')
All inputs are finite; a program needn't handle non-finite values.
Results may differ from a plain program's by a relative error of at most 0.015.
Values may be sent and summed in bfloat16 or wider, within the bound.
A program may use at most 64 MiB of HBM per device.

v0:
```python
import math

import jax
import jax.numpy as jnp
from jax import lax
from jax.sharding import PartitionSpec as P

STEPS = 2


def rebuild_rows(codes, codebooks):
    tok_rows, sub_count = codes.shape
    centroids = codebooks.shape[1]
    sub_width = codebooks.shape[2]
    group_size = min(16, sub_count)
    centroid_ids = jnp.arange(centroids, dtype=jnp.int32)
    diag_eye = jnp.eye(group_size, dtype=jnp.bfloat16)
    pieces = []
    for first_sub in range(0, sub_count, group_size):
        sub_ids = codes[:, first_sub : first_sub + group_size]
        onehot = (sub_ids[:, :, None] == centroid_ids[None, None, :]).astype(jnp.bfloat16)
        onehot = onehot.reshape(tok_rows, group_size * centroids)
        block_table = (
            codebooks[first_sub : first_sub + group_size][:, :, None, :]
            * diag_eye[:, None, :, None]
        )
        block_table = block_table.reshape(group_size * centroids, group_size * sub_width)
        pieces.append(
            jnp.dot(onehot, block_table, preferred_element_type=jnp.float32).astype(jnp.bfloat16)
        )
    return jnp.concatenate(pieces, axis=1)


def contract_rows(left_rows, right_rows):
    return lax.dot_general(
        left_rows, right_rows, (((0,), (0,)), ((), ())), preferred_element_type=jnp.float32
    )


def shards(embeddings, rotation, codes, codebooks):
    tok_rows, model_width = embeddings.shape
    rows_total = tok_rows * lax.axis_size("dp")
    block_rows = model_width // lax.axis_size("dp")
    rotated = jnp.dot(embeddings, rotation, preferred_element_type=jnp.float32)
    rebuilt = rebuild_rows(codes, codebooks)
    rebuilt_wide = rebuilt.astype(jnp.float32)
    residue = rotated - rebuilt_wide
    partial_value = jnp.sum(residue * residue, axis=1)
    row_error = lax.psum(partial_value, "col")
    weights = 1.0 / (1.0 + row_error / (2.0 * model_width))
    weighted = (weights[:, None] * rebuilt_wide).astype(jnp.bfloat16)
    cross_block = lax.psum_scatter(
        contract_rows(embeddings, weighted), "dp", scatter_dimension=0, tiled=True
    )
    start_row = lax.axis_index("dp") * block_rows
    prior_block = lax.dynamic_slice_in_dim(rotation, start_row, block_rows, 0).astype(jnp.float32)
    cross_block = cross_block + 0.2 * rows_total * prior_block
    frob_total = lax.psum(jnp.sum(cross_block * cross_block), ("dp", "col"))
    norm_scale = 1.4 * jnp.sqrt(frob_total / model_width)
    iterate = cross_block / norm_scale
    for step_index in range(STEPS):
        half_iter = iterate.astype(jnp.bfloat16)
        row_panel = lax.all_gather(half_iter, "col", axis=1, tiled=True)
        gram_block = lax.psum_scatter(
            contract_rows(row_panel, half_iter).astype(jnp.bfloat16),
            "dp",
            scatter_dimension=0,
            tiled=True,
        )
        product = jnp.dot(
            row_panel,
            lax.all_gather(gram_block, "dp", axis=0, tiled=True),
            preferred_element_type=jnp.float32,
        )
        iterate = 1.5 * iterate - 0.5 * product
    return math.sqrt(model_width) * iterate


def solution(mesh):
    placed = (P("dp", None), P(None, "col"), P("dp", "col"), P("col", None, None))
    return jax.shard_map(
        shards, mesh=mesh, in_specs=placed, out_specs=P("dp", "col"), check_vma=False
    )
```

profile of v0, /device:TPU:2, one launch (start us, length us, event | category | flops | bytes accessed | tf_op | source)
XLA Modules:
  0.0 1196.6 jit_solution(9498834475879376770)
XLA Ops:
  8.0 1.4 copy.37
  9.6 3.0 iota_compare_fusion.1
  12.6 2.9 copy.36
  15.5 1.5 copy.35
  17.1 3.0 iota_compare_fusion.2
  20.1 2.9 copy.34
  23.0 1.5 copy.33
  24.6 3.0 iota_compare_fusion.3
  27.6 3.0 copy.32
  32.1 3.2 iota_compare_fusion
  35.3 1.6 copy.38
  36.9 2.9 convolution_convert_fusion.3
  39.9 1.5 convolution_convert_fusion.4
  41.7 1.5 convolution_convert_fusion.5
  43.3 1.5 convolution_convert_fusion.2
  46.7 2.4 fusion.1
  49.1 17.7 %psum.14 = f32[512]{0:T(512)S(1)} all-reduce(f32[512]{0:T(512)S(1)} %fusion.1), channel_id=1, replica_groups=mesh['dp'=32,'col'=8] {'col'}, use_global_device_ids=true, to_apply=%region_1.0 | all-reduce | flops 512 | bytes 4096 | tf_op jit(solution)/shard_map/psum | solution.py:49
  66.8 7.8 convolution_bitcast_fusion
  75.7 246.1 %reduce-scatter.4.cloned.1.call-done = f32[128,512]{0,1:T(8,128)} async-done(((f32[4096,512]{0,1:T(8,128)}), f32[128,512]{0,1:T(8,128)}) %reduce-scatter.4.cloned.1.call-update) | async-done | bytes 262160 | tf_op jit(solution)/shard_map/reduce_scatter | solution.py:52
  321.8 1.6 multiply_reduce_fusion
  323.4 93.3 %psum.15 = f32[]{:T(128)} all-reduce(f32[]{:T(128)} %multiply_reduce_fusion), channel_id=1, replica_groups=mesh['dp'=32,'col'=8] {'dp','col'}, use_global_device_ids=true, to_apply=%region_4.0 | all-reduce | flops 1 | bytes 8 | tf_op jit(solution)/shard_map/psum | solution.py:58
  417.4 1.7 fusion.9
  419.3 32.5 %all-gather.5.cloned.1.call-done = bf16[128,4096]{0,1:T(8,128)(2,1)} async-done(((bf16[128,512]{0,1:T(8,128)(2,1)}), bf16[128,4096]{0,1:T(8,128)(2,1)}) %all-gather.5.cloned.1.call-update) | async-done | bytes 1048592 | tf_op jit(solution)/shard_map/all_gather | solution.py:63
  451.8 4.4 convolution_convert_fusion.1
  456.3 217.4 %reduce-scatter.6.cloned.1.call-done = bf16[128,512]{1,0:T(8,128)(2,1)} async-done(((bf16[4096,512]{1,0:T(8,128)(2,1)}), bf16[128,512]{1,0:T(8,128)(2,1)}) %reduce-scatter.6.cloned.1.call-update) | async-done | bytes 131088 | tf_op jit(solution)/shard_map/reduce_scatter | solution.py:64
  673.8 125.9 %all-gather.7.cloned.1.call-done = bf16[4096,512]{1,0:T(8,128)(2,1)} async-done(((bf16[128,512]{1,0:T(8,128)(2,1)}), bf16[4096,512]{1,0:T(8,128)(2,1)}) %all-gather.7.cloned.1.call-update) | async-done | bytes 4194320 | tf_op jit(solution)/shard_map/all_gather | solution.py:72
  799.7 4.6 fusion.14
  804.4 32.4 %all-gather.9.cloned.1.call-done = bf16[128,4096]{0,1:T(8,128)(2,1)} async-done(((bf16[128,512]{0,1:T(8,128)(2,1)}), bf16[128,4096]{0,1:T(8,128)(2,1)}) %all-gather.9.cloned.1.call-update) | async-done | bytes 1048592 | tf_op jit(solution)/shard_map/all_gather | solution.py:63
  836.8 4.4 convolution_convert_fusion
  841.3 219.3 %reduce-scatter.8.cloned.1.call-done = bf16[128,512]{1,0:T(8,128)(2,1)} async-done(((bf16[4096,512]{1,0:T(8,128)(2,1)}), bf16[128,512]{1,0:T(8,128)(2,1)}) %reduce-scatter.8.cloned.1.call-update) | async-done | bytes 131088 | tf_op jit(solution)/shard_map/reduce_scatter | solution.py:64
  1060.6 124.3 %all-gather.11.cloned.1.call-done = bf16[4096,512]{1,0:T(8,128)(2,1)} async-done(((bf16[128,512]{1,0:T(8,128)(2,1)}), bf16[4096,512]{1,0:T(8,128)(2,1)}) %all-gather.11.cloned.1.call-update) | async-done | bytes 4194320 | tf_op jit(solution)/shard_map/all_gather | solution.py:72
  1184.9 3.9 fusion.3
  (55 shorter events, 8.1 us)
Async XLA Ops:
  6.5 2.9 copy-start.10
  6.5 315.2 %reduce-scatter.4.cloned.1.call-start = ((), (), s32[]{:S(2)}) async-start(), calls=%async_computation.3 | async-start | bytes 8650752 | tf_op jit(solution)/shard_map/reduce_scatter | solution.py:52
  30.6 6.3 copy-start.3
  36.9 2.9 copy-start.4
  36.9 2.9 copy-start.7
  39.8 1.6 copy-start.5
  39.8 1.8 copy-start.8
  41.7 1.5 copy-start.9
  43.2 2.2 copy-start.1
  43.2 3.5 copy-start.11
  74.6 377.2 %all-gather.5.cloned.1.call-start = ((), (), s32[]{:S(2)}) async-start(), calls=%async_computation.4 | async-start | bytes 1179648 | tf_op jit(solution)/shard_map/all_gather | solution.py:63
  419.0 254.7 %reduce-scatter.6.cloned.1.call-start = ((), (), s32[]{:S(2)}) async-start(), calls=%async_computation.5 | async-start | bytes 4325376 | tf_op jit(solution)/shard_map/reduce_scatter | solution.py:64
  456.2 343.5 %copy-start.2 = (bf16[128,4096]{0,1:T(8,128)(2,1)S(1)}, bf16[128,4096]{0,1:T(8,128)(2,1)}, u32[]{:S(2)}) copy-start(bf16[128,4096]{0,1:T(8,128)(2,1)} %all-gather.5.cloned.1.call-done) | copy-start | bytes 3145732
  456.2 343.5 %copy-start.6 = (f32[128,512]{0,1:T(8,128)S(1)}, f32[128,512]{0,1:T(8,128)}, u32[]{:S(2)}) copy-start(f32[128,512]{0,1:T(8,128)} %reduce-scatter.4.cloned.1.call-done) | copy-start | bytes 786436
  456.3 343.4 %all-gather.7.cloned.1.call-start = ((), (), s32[]{:S(2)}) async-start(), calls=%async_computation.6 | async-start | bytes 4325376 | tf_op jit(solution)/shard_map/all_gather | solution.py:72
  673.7 163.1 %all-gather.9.cloned.1.call-start = ((), (), s32[]{:S(2)}) async-start(), calls=%async_computation.7 | async-start | bytes 1179648 | tf_op jit(solution)/shard_map/all_gather | solution.py:63
  804.3 256.3 %reduce-scatter.8.cloned.1.call-start = ((), (), s32[]{:S(2)}) async-start(), calls=%async_computation.8 | async-start | bytes 4325376 | tf_op jit(solution)/shard_map/reduce_scatter | solution.py:64
  841.2 343.7 %copy-start = (bf16[128,4096]{0,1:T(8,128)(2,1)S(1)}, bf16[128,4096]{0,1:T(8,128)(2,1)}, u32[]{:S(2)}) copy-start(bf16[128,4096]{0,1:T(8,128)(2,1)} %all-gather.9.cloned.1.call-done) | copy-start | bytes 3145732
  841.3 343.7 %all-gather.11.cloned.1.call-start = ((), (), s32[]{:S(2)}) async-start(), calls=%async_computation.9 | async-start | bytes 4325376 | tf_op jit(solution)/shard_map/all_gather | solution.py:72
Sparse Core Ops, SparseCore 0:
  74.7 247.0 reduce-scatter.3
  419.2 32.5 all-gather.4
  456.4 217.2 reduce-scatter.5
  677.1 122.5 all-gather.6
  804.4 32.3 all-gather.8
  841.4 219.1 reduce-scatter.7
  1064.1 120.7 all-gather.10
where the time goes:
time: 1200 us
  waiting for transfers between devices  998 us (83%)
  blocking collectives  111 us (9%)
  matrix products  35 us (3%)
  local copies, waits for them, and re-layouts  21.9 us (2%)
  other arithmetic  15.8 us (1%)
  between operations  14.4 us (1%)
    reduce_scatter x2, waiting for transfers between devices, shards(): lax.psum_scatter(contract_rows(row_panel, half_iter).astype(jnp.bfloat16)...  437 us
    all_gather x2, waiting for transfers between devices, shards(): lax.all_gather(gram_block, 'dp', axis=0, tiled=True)  250 us
    reduce_scatter x1, waiting for transfers between devices, shards(): lax.psum_scatter(contract_rows(embeddings, weighted), 'dp', scatter_dimen...  246 us
    psum x1, blocking collectives, shards(): frob_total = lax.psum(jnp.sum(cross_block * cross_block), ('dp', 'col'))  93.3 us
    all_gather x2, waiting for transfers between devices, shards(): row_panel = lax.all_gather(half_iter, 'col', axis=1, tiled=True)  64.9 us
  transfers between devices with their start and end apart: 7, of which 7 were waited for; matrix products, arithmetic and copies ran while one was open for 0% of the time, Pallas kernels for 0%

commit v1 on v0

v1 whole, which is shorter than its diff:
```python
import functools
import math

import jax
import jax.numpy as jnp
from jax import lax
from jax.experimental import pallas as pl
from jax.experimental.pallas import tpu as pltpu
from jax.sharding import PartitionSpec as P

MESH = pl.DeviceIdType.MESH
BF = jnp.bfloat16
F32 = jnp.float32
NX, NY, NZH, NZL, NC = 4, 4, 2, 4, 2
NSEM = 256


def rebuild_rows(codes, codebooks):
    tok_rows, sub_count = codes.shape
    centroids = codebooks.shape[1]
    sub_width = codebooks.shape[2]
    group_size = min(16, sub_count)
    centroid_ids = jnp.arange(centroids, dtype=jnp.int32)
    diag_eye = jnp.eye(group_size, dtype=jnp.bfloat16)
    pieces = []
    for first_sub in range(0, sub_count, group_size):
        sub_ids = codes[:, first_sub : first_sub + group_size]
        onehot = (sub_ids[:, :, None] == centroid_ids[None, None, :]).astype(jnp.bfloat16)
        onehot = onehot.reshape(tok_rows, group_size * centroids)
        block_table = (
            codebooks[first_sub : first_sub + group_size][:, :, None, :]
            * diag_eye[:, None, :, None]
        )
        block_table = block_table.reshape(group_size * centroids, group_size * sub_width)
        pieces.append(
            jnp.dot(onehot, block_table, preferred_element_type=jnp.float32).astype(jnp.bfloat16)
        )
    return jnp.concatenate(pieces, axis=1)


def dot_nt(a, b):
    return lax.dot_general(a, b, (((1,), (1,)), ((), ())), preferred_element_type=F32)


def dot_nn(a, b):
    return jnp.dot(a, b, preferred_element_type=F32)


class Place:
    def __init__(self):
        dp, col = lax.axis_index("dp"), lax.axis_index("col")
        self.x = dp // (NZH * NY)
        self.zh = (dp // NY) % NZH
        self.y = dp % NY
        self.zl = col // NC
        self.c = col % NC
        self.z = self.zh * NZL + self.zl

    def at(self, dx=0, dy=0, dz=0, dc=0):
        x = (self.x + dx) % NX
        y = (self.y + dy) % NY
        z = (self.z + dz) % (NZH * NZL)
        c = (self.c + dc) % NC
        return (x * (NZH * NY) + (z // NZL) * NY + y, (z % NZL) * NC + c)

    def along(self, axis, step):
        return self.at(dx=step) if axis == "x" else self.at(dy=step)

    def index(self, axis):
        return self.x if axis == "x" else self.y


class Sems:
    def __init__(self, send, recv):
        self.send, self.recv, self.used = send, recv, 0

    def take(self, count=1):
        base = self.used
        self.used += count
        assert self.used <= NSEM
        return base

    def copy(self, src, dst, index, device):
        return pltpu.make_async_remote_copy(
            src_ref=src,
            dst_ref=dst,
            send_sem=self.send.at[index],
            recv_sem=self.recv.at[index],
            device_id=device,
            device_id_type=MESH,
        )


def ring_scatter(place, sems, axis, chunk, out, keep, diag, got, to_r, to_l, from_l, from_r):
    rows = diag.shape[0]
    half = rows // 2
    lo, hi = pl.ds(0, half), pl.ds(half, half)
    p = place.index(axis)
    right, left = place.along(axis, 1), place.along(axis, -1)
    s = sems.take(6)
    chunk((p + 2) % 4)
    diag[...] = keep[...].astype(BF)
    c0 = sems.copy(diag.at[lo], got.at[lo], s, right)
    c1 = sems.copy(diag.at[hi], got.at[hi], s + 1, left)
    c0.start()
    c1.start()
    yield
    chunk((p + 1) % 4)
    to_r[hi] = keep[hi].astype(BF)
    c2 = sems.copy(to_r.at[hi], from_l.at[hi], s + 2, right)
    c2.start()
    c0.wait_recv()
    to_r[lo] = (keep[lo] + got[lo].astype(F32)).astype(BF)
    c3 = sems.copy(to_r.at[lo], from_l.at[lo], s + 3, right)
    c3.start()
    yield
    chunk((p + 3) % 4)
    to_l[lo] = keep[lo].astype(BF)
    c4 = sems.copy(to_l.at[lo], from_r.at[lo], s + 4, left)
    c4.start()
    c1.wait_recv()
    to_l[hi] = (keep[hi] + got[hi].astype(F32)).astype(BF)
    c5 = sems.copy(to_l.at[hi], from_r.at[hi], s + 5, left)
    c5.start()
    yield
    chunk(p)
    for c in (c2, c3, c4, c5):
        c.wait_recv()
    out[...] = keep[...] + from_l[...].astype(F32) + from_r[...].astype(F32)
    for c in (c0, c1, c2, c3, c4, c5):
        c.wait_send()
    yield


def ring_gather(place, sems, axis, buf):
    half = buf.shape[1] // 2
    lo, hi = pl.ds(0, half), pl.ds(half, half)
    p = place.index(axis)
    right, left = place.along(axis, 1), place.along(axis, -1)
    s = sems.take(4)
    before, after = (p + 3) % 4, (p + 1) % 4
    c0 = sems.copy(buf.at[p], buf.at[p], s, right)
    c1 = sems.copy(buf.at[p], buf.at[p], s + 1, left)
    c0.start()
    c1.start()
    yield
    c0.wait_recv()
    c2 = sems.copy(buf.at[before, lo], buf.at[before, lo], s + 2, right)
    c2.start()
    c1.wait_recv()
    c3 = sems.copy(buf.at[after, hi], buf.at[after, hi], s + 3, left)
    c3.start()
    yield
    c2.wait_recv()
    c3.wait_recv()
    for c in (c0, c1, c2, c3):
        c.wait_send()
    yield


def run(*gens):
    live = list(gens)
    while live:
        for g in list(live):
            try:
                next(g)
            except StopIteration:
                live.remove(g)


def spread_z(place, sems, bt, at):
    z, c = place.z, place.c
    d = (place.zl - place.y + 4) % 4
    back = (4 - d) % 4
    up, down, other = place.at(dz=1), place.at(dz=-1), place.at(dc=1)
    up_origin = ((z - d + 8) % 8) // 4
    down_origin = ((z + back) % 8) // 4
    half = at.shape[3] // 2
    lo, hi = pl.ds(0, half), pl.ds(half, half)
    far = 1 - place.zh
    s_up, s_down = sems.take(4), sems.take(4)
    s_up_half, s_down_half = sems.take(4), sems.take(4)
    s_core = sems.take(8)

    def core_copy(origin, q):
        return sems.copy(at.at[origin, c, q], at.at[origin, c, q], s_core + origin * 4 + q, other)

    @pl.when(d == 0)
    def _():
        at[place.zh, c] = bt[...]

    def up_full(q):
        return sems.copy(at.at[up_origin, c, q], at.at[up_origin, c, q], s_up + q, up)

    def down_full(q):
        return sems.copy(at.at[down_origin, c, q], at.at[down_origin, c, q], s_down + q, down)

    def up_half(q):
        return sems.copy(at.at[up_origin, c, q, lo], at.at[up_origin, c, q, lo], s_up_half + q, up)

    def down_half(q):
        return sems.copy(at.at[down_origin, c, q, hi], at.at[down_origin, c, q, hi], s_down_half + q, down)

    for t in range(8):
        q_up = t - d

        @pl.when((q_up >= 0) & (q_up < 4))
        def _(q_up=q_up):
            @pl.when(d > 0)
            def _():
                up_full(q_up).wait_recv()

            @pl.when(d < 3)
            def _():
                up_full(q_up).start()

            @pl.when(d == 3)
            def _():
                up_half(q_up).start()

            core_copy(up_origin, q_up).start()

        q_down = t - back

        @pl.when((q_down >= 0) & (q_down < 4))
        def _(q_down=q_down):
            @pl.when(d > 0)
            def _():
                down_full(q_down).wait_recv()

            @pl.when(d != 1)
            def _():
                down_full(q_down).start()

            @pl.when(d == 1)
            def _():
                down_half(q_down).start()

            @pl.when(d > 0)
            def _():
                core_copy(down_origin, q_down).start()

        if t >= 4:

            @pl.when(d == 0)
            def _(q=t - 4):
                sems.copy(at.at[far, c, q, lo], at.at[far, c, q, lo], s_up_half + q, up).wait_recv()
                sems.copy(at.at[far, c, q, hi], at.at[far, c, q, hi], s_down_half + q, down).wait_recv()
                core_copy(far, q).start()

    for origin in range(2):
        for q in range(4):
            pltpu.make_async_remote_copy(
                src_ref=at.at[origin, 1 - c, q],
                dst_ref=at.at[origin, 1 - c, q],
                send_sem=sems.send.at[s_core + origin * 4 + q],
                recv_sem=sems.recv.at[s_core + origin * 4 + q],
                device_id=other,
                device_id_type=MESH,
            ).wait()
    for q in range(4):

        @pl.when(d < 3)
        def _(q=q):
            up_full(q).wait_send()

        @pl.when(d == 3)
        def _(q=q):
            up_half(q).wait_send()

        @pl.when(d != 1)
        def _(q=q):
            down_full(q).wait_send()

        @pl.when(d == 1)
        def _(q=q):
            down_half(q).wait_send()


def share_sum(place, sems, mine, slots, partners):
    s = sems.take(len(partners))
    copies = [sems.copy(mine, slots.at[i], s + i, device) for i, device in enumerate(partners)]
    for c in copies:
        c.start()
    return copies


def finish_sum(copies, mine, slots):
    for c in copies:
        c.wait()
    total = mine[...]
    for i in range(len(copies)):
        total = total + slots[i]
    return total


def main_kernel(
    prior_scale, width, wt, e, prior, out,
    keep_a, keep_b, big, small, own_a, own_b, ab, ab_out, ab_in, xo, red,
    bt, at, gkeep, gbuf, gown, gfull, ykeep, ybuf, sq, sq_in, last_out, last_in,
    send, recv,
):
    place = Place()
    sems = Sems(send, recv)
    barrier = pltpu.get_barrier_semaphore()
    partners = (
        [place.at(dx=i) for i in (1, 2, 3)]
        + [place.at(dy=i) for i in (1, 2, 3)]
        + [place.at(dz=i) for i in range(1, 8)]
        + [place.at(dc=1)]
    )
    for device in partners:
        pl.semaphore_signal(barrier, inc=1, device_id=device, device_id_type=MESH)
    pl.semaphore_wait(barrier, len(partners))

    block = out.shape[2]
    n_half = wt.shape[0] // 2
    x_cols = e.shape[1] // NX

    def chunk_a(xi):
        start = pl.multiple_of(xi * x_cols, x_cols)
        value = dot_nn(wt[0:n_half], e[:, pl.ds(start, x_cols)])
        for zh in range(NZH):
            for y in range(NY):
                at_in, at_out = (zh * NY + y) * block, (y * NZH + zh) * block
                keep_a[:, at_out : at_out + block] = value[:, at_in : at_in + block]

    def chunk_b(yi):
        parts = []
        for x in range(NX):
            for zh in range(NZH):
                start = pl.multiple_of(x * x_cols + (zh * NY + yi) * block, block)
                parts.append(e[:, pl.ds(start, block)])
        keep_b[...] = dot_nn(wt[n_half:], jnp.concatenate(parts, axis=1))

    def piece(source, keep):
        def chunk(i):
            width_of = keep.shape[1]
            keep[...] = source[:, pl.ds(pl.multiple_of(i * width_of, width_of), width_of)]

        return chunk

    run(
        ring_scatter(place, sems, "x", chunk_a, own_a, keep_a, *[big.at[0, i] for i in range(6)]),
        ring_scatter(place, sems, "y", chunk_b, own_b, keep_b, *[big.at[1, i] for i in range(6)]),
    )
    run(
        ring_scatter(place, sems, "y", piece(own_a, red.at[0]), ab.at[0], red.at[0], *[small.at[0, i] for i in range(6)]),
        ring_scatter(place, sems, "x", piece(own_b, red.at[1]), ab.at[1], red.at[1], *[small.at[1, i] for i in range(6)]),
    )
    ab_out[...] = ab[1 - place.zh].astype(BF)
    s = sems.take()
    swap = sems.copy(ab_out, ab_in, s, place.at(dz=4))
    swap.start()
    swap.wait()
    x_new = ab[place.zh] + ab_in[...].astype(F32) + prior_scale * prior[...]
    xo[...] = x_new
    squares = x_new * x_new
    folded = jnp.sum(squares.reshape(squares.shape[0] // 8, 8, squares.shape[1]), axis=0)
    part = folded[:, 0:128]
    for i in range(1, folded.shape[1] // 128):
        part = part + folded[:, i * 128 : (i + 1) * 128]
    sq[0] = part

    y_copies = share_sum(place, sems, sq.at[0], sq_in.at[0], [place.at(dy=i) for i in (1, 2, 3)])
    inv = None
    for step in range(2):
        b_ref, a_ref, g_ref = bt.at[step], at.at[step], gfull.at[step]
        b_ref[place.y] = xo[...].astype(BF)
        run(ring_gather(place, sems, "y", b_ref))
        if step == 0:
            sq[1] = finish_sum(y_copies, sq.at[0], sq_in.at[0])
            z_copies = share_sum(place, sems, sq.at[1], sq_in.at[1], [place.at(dz=i) for i in range(1, 8)])
        spread_z(place, sems, b_ref, a_ref)
        if step == 0:
            sq[2] = finish_sum(z_copies, sq.at[1], sq_in.at[1])
            c_copies = share_sum(place, sems, sq.at[2], sq_in.at[2], [place.at(dc=1)])
        for i in range(NZH * NC):
            total = None
            for q in range(NY):
                term = dot_nt(b_ref[q], a_ref[i // NC, i % NC, q])
                total = term if total is None else total + term
            w = total.shape[1]
            gkeep[0, :, i * w : (i + 1) * w] = total
        g_rows = gkeep.shape[1] // NX

        def chunk_g(xi):
            gkeep[1, 0:g_rows] = gkeep[0, pl.ds(pl.multiple_of(xi * g_rows, g_rows), g_rows)]

        run(
            ring_scatter(
                place, sems, "x", chunk_g, gown, gkeep.at[1, 0:g_rows], *[gbuf.at[step, i] for i in range(6)]
            )
        )
        if step == 0:
            sq[3] = finish_sum(c_copies, sq.at[2], sq_in.at[2])
            x_copies = share_sum(place, sems, sq.at[3], sq_in.at[3], [place.at(dx=i) for i in (1, 2, 3)])
        g_ref[place.x] = gown[...].astype(BF)
        run(ring_gather(place, sems, "x", g_ref))
        if step == 0:
            total = jnp.sum(finish_sum(x_copies, sq.at[3], sq_in.at[3]))
            scale2 = jnp.full((8, 128), 1.96 / width, F32) * total
            inv = 1.0 / jnp.sqrt(scale2)
        gram = jnp.concatenate([g_ref[i] for i in range(NX)], axis=0)

        def chunk_y(q):
            value = None
            for i in range(NZH * NC):
                w = a_ref.shape[3]
                term = dot_nn(gram[:, i * w : (i + 1) * w], a_ref[i // NC, i % NC, q])
                value = term if value is None else value + term
            ykeep[...] = value

        run(ring_scatter(place, sems, "y", chunk_y, red.at[0], ykeep, *[ybuf.at[step, i] for i in range(6)]))
        if step == 0:
            f = jnp.tile(inv[0:1], (1, xo.shape[1] // 128))
            xo[...] = (1.5 * xo[...] - 0.5 * (red[0] * (f * f))) * f
        else:
            xo[...] = math.sqrt(width) * (1.5 * xo[...] - 0.5 * red[0])
    s = sems.take()
    mine = pl.ds(pl.multiple_of(place.zh * block, block), block)
    theirs = pl.ds(pl.multiple_of((1 - place.zh) * block, block), block)
    last_out[...] = xo[:, theirs].astype(last_out.dtype)
    swap = sems.copy(last_out, last_in, s, place.at(dz=4))
    swap.start()
    out[place.zh] = xo[:, mine]
    swap.wait()
    out[1 - place.zh] = last_in[...].astype(F32)


def shards(embeddings, rotation, codes, codebooks):
    tok_rows, width = embeddings.shape
    cols = rotation.shape[1]
    rows_total = tok_rows * lax.axis_size("dp")
    block = width // lax.axis_size("dp")
    rotated = jnp.dot(embeddings, rotation, preferred_element_type=jnp.float32)
    rebuilt = rebuild_rows(codes, codebooks)
    rebuilt_wide = rebuilt.astype(jnp.float32)
    residue = rotated - rebuilt_wide
    row_error = lax.psum(jnp.sum(residue * residue, axis=1), "col")
    weights = 1.0 / (1.0 + row_error / (2.0 * width))
    weighted_t = (weights[:, None] * rebuilt_wide).astype(BF).T
    place = Place()
    panels = rotation.reshape(NX, NZH, NY, block, NZH, cols // NZH)
    prior = lax.dynamic_index_in_dim(panels, place.x, 0, keepdims=False)
    prior = lax.dynamic_index_in_dim(prior, place.y, 1, keepdims=False)
    prior = lax.dynamic_index_in_dim(prior, place.zh, 2, keepdims=False)
    n = cols // NZH
    m = NZH * block
    prior = prior.reshape(m, n).T.astype(F32)
    panel = m * NY
    wide = n * NZH * NC
    vm = pltpu.VMEM
    out_t = pl.pallas_call(
        functools.partial(main_kernel, 0.2 * rows_total, width),
        out_shape=jax.ShapeDtypeStruct((NZH, n, block), F32),
        in_specs=[pl.BlockSpec(memory_space=pltpu.VMEM)] * 3,
        out_specs=pl.BlockSpec(memory_space=pltpu.VMEM),
        scratch_shapes=[
            vm((n, panel), F32), vm((n, panel), F32),
            vm((2, 6, n, panel), BF), vm((2, 6, n, m), BF),
            vm((n, panel), F32), vm((n, panel), F32),
            vm((2, n, m), F32), vm((n, m), BF), vm((n, m), BF),
            vm((n, m), F32), vm((2, n, m), F32),
            vm((2, NY, n, m), BF), vm((2, NZH, NC, NY, n, m), BF),
            vm((2, n, wide), F32), vm((2, 6, n // NX, wide), BF), vm((n // NX, wide), F32),
            vm((2, NX, n // NX, wide), BF),
            vm((n, m), F32), vm((2, 6, n, m), BF),
            vm((4, 8, 128), F32), vm((4, 7, 8, 128), F32),
            vm((n, block), BF), vm((n, block), BF),
            pltpu.SemaphoreType.DMA((NSEM,)), pltpu.SemaphoreType.DMA((NSEM,)),
        ],
        compiler_params=pltpu.CompilerParams(collective_id=0, has_side_effects=True, vmem_limit_bytes=60 * 2**20),
        name="main",
    )(weighted_t, embeddings, prior)
    return out_t.reshape(cols, block).T


def solution(mesh):
    placed = (P("dp", None), P(None, "col"), P("dp", "col"), P("col", None, None))
    return jax.shard_map(
        shards, mesh=mesh, in_specs=placed, out_specs=P("dp", "col"), check_vma=False
    )
```

time: 1200 us -> 243 us (0.20)
  waiting for transfers between devices: 998 us -> 0 us
  Pallas kernels: 0 us -> 179 us
  blocking collectives: 111 us -> 17.7 us
  matrix products: 35 us -> 9.13 us
  between operations: 14.4 us -> 0.27 us
    reduce_scatter x3 -> x0, waiting for transfers between devices: 683 us -> none  [the longest x2 437 us: shards(): lax.psum_scatter(contract_rows(row_panel, half_iter).astype(jnp.bfloat16)...]
    all_gather x4 -> x0, waiting for transfers between devices: 315 us -> none  [the longest x2 250 us: shards(): lax.all_gather(gram_block, 'dp', axis=0, tiled=True)]
    pallas_call x0 -> x1, Pallas kernels: none -> 179 us  [shards(): pl.pallas_call(functools.partial(main_kernel, 0.2 * rows_total, width), o...]
    psum x2 -> x1, blocking collectives: 111 us -> 17.7 us  [shards(): row_error = lax.psum(jnp.sum(residue * residue, axis=1), 'col')]
    dot_general x5 -> x0, matrix products: 25.2 us -> none  [the longest x3 16.7 us: contract_rows(): lax.dot_general(left_rows, right_rows, (((0,), (0,)), ((), ())), preferre...]
  transfers between devices with their start and end apart: 7 -> 0, of which waited for: 7 -> 0; matrix products, arithmetic and copies ran while one was open for 0% -> 0% of each run, Pallas kernels for 0% -> 0%
where the time goes in v1:
time: 243 us; the launch traced here: 242 us
  Pallas kernels  179 us (74%)
  local copies, waits for them, and re-layouts  22.2 us (9%)
  blocking collectives  17.7 us (7%)
  other arithmetic  13.5 us (6%)
  matrix products  9.13 us (4%)
    pallas_call x1, Pallas kernels, shards(): pl.pallas_call(functools.partial(main_kernel, 0.2 * rows_total, width), o...  179 us
    psum x1, blocking collectives, shards(): row_error = lax.psum(jnp.sum(residue * residue, axis=1), 'col')  17.7 us
    eq x4, other arithmetic, rebuild_rows(): sub_ids[:, :, None] == centroid_ids[None, None, :]  12.1 us
    unnamed x18, local copies, waits for them, and re-layouts  10.9 us
    reshape x1, local copies, waits for them, and re-layouts, shards(): panels = rotation.reshape(NX, NZH, NY, block, NZH, cols // NZH)  6.91 us
    dot_general x4, matrix products, rebuild_rows(): jnp.dot(onehot, block_table, preferred_element_type=jnp.float32)  6.74 us

profile of v1, /device:TPU:2, one launch (start us, length us, event | category | flops | bytes accessed | tf_op | source)
XLA Modules:
  0.0 241.9 jit_solution(10287111424587044190)
XLA Ops:
  0.0 0.8 fusion.6
  0.8 0.1 copy.21
  0.9 3.0 %iota_compare_fusion = pred[512,16,256]{2,1,0:T(8,128)(4,1)S(1)} fusion(s32[512,16]{1,0:T(8,128)S(1)} %copy.21), kind=kLoop, calls=%fused_computation | loop fusion | flops 2097152 | bytes 2129920 | tf_op jit(solution)/shard_map/eq | solution.py:28
  4.0 1.6 copy.32
  5.7 0.4 multiply_bitcast_fusion.3
  6.1 0.4 copy.33
  6.5 2.2 convolution_convert_fusion
  8.8 3.0 %iota_compare_fusion.1 = pred[512,16,256]{2,1,0:T(8,128)(4,1)S(1)} fusion(s32[512,16]{1,0:T(8,128)S(1)} %copy.19), kind=kLoop, calls=%fused_computation.1 | loop fusion | flops 2097152 | bytes 2129920 | tf_op jit(solution)/shard_map/eq | solution.py:28
  11.8 1.6 copy.30
  13.4 0.4 copy.31
  13.8 1.5 convolution_convert_fusion.1
  15.4 0.1 copy.17
  15.5 3.0 %iota_compare_fusion.2 = pred[512,16,256]{2,1,0:T(8,128)(4,1)S(1)} fusion(s32[512,16]{1,0:T(8,128)S(1)} %copy.17), kind=kLoop, calls=%fused_computation.2 | loop fusion | flops 2097152 | bytes 2129920 | tf_op jit(solution)/shard_map/eq | solution.py:28
  18.5 1.6 copy.28
  20.1 0.4 copy.29
  20.5 1.5 convolution_convert_fusion.2
  22.1 0.1 copy.15
  22.2 3.2 %iota_compare_fusion.3 = pred[512,16,256]{2,1,0:T(8,128)(4,1)S(1)} fusion(s32[512,16]{1,0:T(8,128)S(1)} %copy.15), kind=kLoop, calls=%fused_computation.3 | loop fusion | flops 2097152 | bytes 2129920 | tf_op jit(solution)/shard_map/eq | solution.py:28
  25.4 1.6 copy.26
  27.0 0.4 copy.27
  27.4 1.5 convolution_convert_fusion.3
  29.0 0.6 copy-done
  29.6 1.3 copy-done.1
  30.9 2.4 fusion.1
  33.3 17.7 %psum.7 = f32[512]{0:T(512)S(1)} all-reduce(f32[512]{0:T(512)S(1)} %fusion.1), channel_id=1, replica_groups=mesh['dp'=32,'col'=8] {'col'}, use_global_device_ids=true, to_apply=%region_1.0 | all-reduce | flops 512 | bytes 4096 | tf_op jit(solution)/shard_map/psum | solution.py:440
  50.9 0.9 fusion.3.wt
  51.8 6.9 %reshape.215 = bf16[4,2,4,128,2,256]{5,4,3,2,1,0:T(2,128)(2,1)} reshape(bf16[4096,512]{1,0:T(8,128)(2,1)} %param.5) | data formatting | bytes 8388608 | tf_op jit(solution)/shard_map/reshape | solution.py:444
  58.7 1.2 constant_dynamic-slice_fusion
  59.9 0.2 copy.25
  60.2 0.7 copy.36
  60.9 179.1 %main.1 = f32[2,256,128]{2,1,0:T(8,128)} custom-call(bf16[512,512]{1,0:T(8,128)(2,1)} %fusion.3.wt, bf16[512,4096]{1,0:T(8,128)(2,1)} %e.1, f32[256,256]{1,0:T(8,128)} %bitcast.64), custom_call_target="tpu_custom_call" | custom-call | tf_op jit(solution)/shard_map/main/pallas_call | solution.py:454
  240.1 1.8 copy.24
  (15 shorter events, 0.3 us)
Async XLA Ops:
  3.9 1.6 copy-start.2
  27.4 2.2 copy-start
  27.4 3.5 %copy-start.1 = (bf16[4096,512]{1,0:T(8,128)(2,1)S(1)}, bf16[4096,512]{1,0:T(8,128)(2,1)}, u32[]{:S(2)}) copy-start(bf16[4096,512]{1,0:T(8,128)(2,1)} %param.5) | copy-start | bytes 12582916
  27.4 3.5 %copy-start.3 = (bf16[512,128]{0,1:T(8,128)(2,1)S(1)}, bf16[512,128]{0,1:T(8,128)(2,1)}, u32[]{:S(2)}) copy-start(bf16[512,128]{0,1:T(8,128)(2,1)} %convolution_convert_fusion) | copy-start | bytes 393220

commit v2 on v1

v2 whole, which is shorter than its diff:
```python
import functools
import math

import jax
import jax.numpy as jnp
from jax import lax
from jax.experimental import pallas as pl
from jax.experimental.pallas import tpu as pltpu
from jax.sharding import PartitionSpec as P

MESH = pl.DeviceIdType.MESH
BF = jnp.bfloat16
F32 = jnp.float32
NX, NY, NZH, NZL, NC = 4, 4, 2, 4, 2
NSEM = 480


def rebuild_kernel(codes, table, out):
    lanes = 128

    def one_subspace(m, carry):
        entries = table[m].astype(F32)
        ids = codes[pl.ds(m, 1), :]
        for first in range(0, codes.shape[1], lanes):
            index = jnp.broadcast_to(ids[:, first : first + lanes], (entries.shape[0], lanes))
            within = index % lanes
            value = None
            for part in range(entries.shape[1] // lanes):
                picked = jnp.take_along_axis(
                    entries[:, part * lanes : (part + 1) * lanes], within, axis=1, mode="promise_in_bounds"
                )
                value = picked if value is None else jnp.where(index >= part * lanes, picked, value)
            out[m, :, first : first + lanes] = value
        return carry

    lax.fori_loop(0, codes.shape[0], one_subspace, 0, unroll=4)


def dot_nt(a, b):
    return lax.dot_general(a, b, (((1,), (1,)), ((), ())), preferred_element_type=F32)


def dot_nn(a, b):
    return jnp.dot(a, b, preferred_element_type=F32)


class Place:
    def __init__(self):
        dp, col = lax.axis_index("dp"), lax.axis_index("col")
        self.x = dp // (NZH * NY)
        self.zh = (dp // NY) % NZH
        self.y = dp % NY
        self.zl = col // NC
        self.c = col % NC
        self.z = self.zh * NZL + self.zl

    def at(self, dx=0, dy=0, dz=0, dc=0):
        x = (self.x + dx) % NX
        y = (self.y + dy) % NY
        z = (self.z + dz) % (NZH * NZL)
        c = (self.c + dc) % NC
        return (x * (NZH * NY) + (z // NZL) * NY + y, (z % NZL) * NC + c)

    def col_peer(self, i):
        return (lax.axis_index("dp"), (lax.axis_index("col") + i) % (NZL * NC))

    def other_end(self, i):
        zl = (self.zl + i) % NZL
        return (self.x * (NZH * NY) + (1 - self.zh) * NY + self.y, zl * NC + self.c)

    def along(self, axis, step):
        return self.at(dx=step) if axis == "x" else self.at(dy=step)

    def index(self, axis):
        return self.x if axis == "x" else self.y


class Sems:
    def __init__(self, send, recv):
        self.send, self.recv, self.used = send, recv, 0

    def take(self, count=1):
        base = self.used
        self.used += count
        assert self.used <= NSEM
        return base

    def copy(self, src, dst, index, device):
        return pltpu.make_async_remote_copy(
            src_ref=src,
            dst_ref=dst,
            send_sem=self.send.at[index],
            recv_sem=self.recv.at[index],
            device_id=device,
            device_id_type=MESH,
        )


def ring_scatter(place, sems, axis, chunk, out, keep, diag, got, to_r, to_l, from_l, from_r):
    rows = diag.shape[0]
    half = rows // 2
    lo, hi = pl.ds(0, half), pl.ds(half, half)
    p = place.index(axis)
    right, left = place.along(axis, 1), place.along(axis, -1)
    s = sems.take(6)
    chunk((p + 2) % 4)
    diag[...] = keep[...].astype(BF)
    c0 = sems.copy(diag.at[lo], got.at[lo], s, right)
    c1 = sems.copy(diag.at[hi], got.at[hi], s + 1, left)
    c0.start()
    c1.start()
    yield
    chunk((p + 1) % 4)
    to_r[hi] = keep[hi].astype(BF)
    c2 = sems.copy(to_r.at[hi], from_l.at[hi], s + 2, right)
    c2.start()
    c0.wait_recv()
    to_r[lo] = (keep[lo] + got[lo].astype(F32)).astype(BF)
    c3 = sems.copy(to_r.at[lo], from_l.at[lo], s + 3, right)
    c3.start()
    yield
    chunk((p + 3) % 4)
    to_l[lo] = keep[lo].astype(BF)
    c4 = sems.copy(to_l.at[lo], from_r.at[lo], s + 4, left)
    c4.start()
    c1.wait_recv()
    to_l[hi] = (keep[hi] + got[hi].astype(F32)).astype(BF)
    c5 = sems.copy(to_l.at[hi], from_r.at[hi], s + 5, left)
    c5.start()
    yield
    chunk(p)
    for c in (c2, c3, c4, c5):
        c.wait_recv()
    out[...] = keep[...] + from_l[...].astype(F32) + from_r[...].astype(F32)
    for c in (c0, c1, c2, c3, c4, c5):
        c.wait_send()


def ring_gather(place, sems, axis, buf, first=0, rows=None):
    rows = buf.shape[1] if rows is None else rows
    half = rows // 2
    all_rows, lo, hi = pl.ds(first, rows), pl.ds(first, half), pl.ds(first + half, half)
    p = place.index(axis)
    right, left = place.along(axis, 1), place.along(axis, -1)
    s = sems.take(4)
    before, after = (p + 3) % 4, (p + 1) % 4
    c0 = sems.copy(buf.at[p, all_rows], buf.at[p, all_rows], s, right)
    c1 = sems.copy(buf.at[p, all_rows], buf.at[p, all_rows], s + 1, left)
    c0.start()
    c1.start()
    yield
    c0.wait_recv()
    c2 = sems.copy(buf.at[before, lo], buf.at[before, lo], s + 2, right)
    c2.start()
    c1.wait_recv()
    c3 = sems.copy(buf.at[after, hi], buf.at[after, hi], s + 3, left)
    c3.start()
    yield
    c2.wait_recv()
    c3.wait_recv()
    for c in (c0, c1, c2, c3):
        c.wait_send()


def run(*gens):
    live = list(gens)
    while live:
        pump(live)


def pump(live):
    for g in list(live):
        if next(g, live) is live:
            live.remove(g)


class Spread:
    def __init__(self, place, sems, bt, at):
        self.place, self.sems, self.bt, self.at = place, sems, bt, at
        z = place.z
        self.d = (place.zl - place.y + 4) % 4
        self.back = (4 - self.d) % 4
        self.up, self.down, self.other = place.at(dz=1), place.at(dz=-1), place.at(dc=1)
        self.up_origin = ((z - self.d + 8) % 8) // 4
        self.down_origin = ((z + self.back) % 8) // 4
        self.parts, self.slots = at.shape[0], at.shape[1]
        self.rows = at.shape[4]
        self.count = self.parts * self.slots
        n = self.count
        self.s_up, self.s_down = sems.take(n), sems.take(n)
        self.s_up_half, self.s_down_half = sems.take(n), sems.take(n)
        self.s_core = sems.take(2 * n)

    def spot(self, origin, n, part=None):
        ref = self.at.at[n // self.slots, n % self.slots, origin, self.place.c]
        half = self.rows // 2
        if part is not None:
            ref = ref.at[pl.ds(part * half, half)]
        return ref

    def source(self, n):
        first = pl.multiple_of((n // self.slots) * self.rows, self.rows)
        return self.bt.at[n % self.slots, pl.ds(first, self.rows)]

    def full(self, up, n, from_source=False):
        origin = self.up_origin if up else self.down_origin
        src = self.source(n) if from_source else self.spot(origin, n)
        base, device = (self.s_up, self.up) if up else (self.s_down, self.down)
        return self.sems.copy(src, self.spot(origin, n), base + n, device)

    def half(self, up, n, origin):
        part = 0 if up else 1
        base, device = (self.s_up_half, self.up) if up else (self.s_down_half, self.down)
        return self.sems.copy(self.spot(origin, n, part), self.spot(origin, n, part), base + n, device)

    def core(self, origin, n, from_source=False):
        src = self.source(n) if from_source else self.spot(origin, n)
        return self.sems.copy(src, self.spot(origin, n), self.s_core + origin * self.count + n, self.other)

    def steps(self, first, last):
        d, n_all, far = self.d, self.count, 1 - self.place.zh

        def slot(t, carry):
            @pl.when((d == 0) & (t < n_all))
            def _():
                self.full(True, t, True).start()
                self.full(False, t, True).start()
                self.core(self.place.zh, t, True).start()

            for up, lag, last_d in ((True, d, 3), (False, self.back, 1)):
                origin = self.up_origin if up else self.down_origin
                n = t - lag

                @pl.when((d > 0) & (n >= 0) & (n < n_all))
                def _(up=up, n=n, last_d=last_d, origin=origin):
                    self.full(up, n).wait_recv()

                    @pl.when(d != last_d)
                    def _():
                        self.full(up, n).start()

                    @pl.when(d == last_d)
                    def _():
                        self.half(up, n, origin).start()

                    self.core(origin, n).start()

            n = t - 4

            @pl.when((d == 0) & (n >= 0))
            def _():
                self.half(True, n, far).wait_recv()
                self.half(False, n, far).wait_recv()
                self.core(far, n).start()

            return carry

        lax.fori_loop(first, last, slot, 0)

    def arrived(self, r):
        for q in range(self.slots):
            for origin in range(2):
                self.core(origin, r * self.slots + q).wait_recv()

        @pl.when(self.d == 0)
        def _():
            for q in range(self.slots):
                rows = pl.ds(r * self.rows, self.rows)
                self.at[r, q, self.place.zh, self.place.c] = self.bt[q, rows]

    def sent(self):
        d = self.d

        def one(n, carry):
            for up, last_d in ((True, 3), (False, 1)):
                origin = self.up_origin if up else self.down_origin

                @pl.when(d != last_d)
                def _(up=up):
                    self.full(up, n).wait_send()

                @pl.when(d == last_d)
                def _(up=up, origin=origin):
                    self.half(up, n, origin).wait_send()

            for origin in range(2):
                self.core(origin, n).wait_send()
            return carry

        lax.fori_loop(0, self.count, one, 0)


def share_sum(place, sems, mine, slots, partners):
    s = sems.take(len(partners))
    copies = [sems.copy(mine, slots.at[i], s + i, device) for i, device in enumerate(partners)]
    for c in copies:
        c.start()
    return copies


def finish_sum(copies, mine, slots):
    for c in copies:
        c.wait()
    total = mine[...]
    for i in range(len(copies)):
        total = total + slots[i]
    return total


def main_kernel(
    prior_scale, width, rebuilt, e, rot, out,
    wt, err, err_in, keep_a, keep_b, big, small, own_a, own_b, ab, ab_out, ab_in, xo, red,
    bt, at, gkeep, gtake, gbuf, gown, gfull, ykeep, ybuf, sq, sq_in, last_out, last_in,
    send, recv,
):
    place = Place()
    sems = Sems(send, recv)
    barrier = pltpu.get_barrier_semaphore()
    col_peers = [place.col_peer(i) for i in range(1, NZL * NC)]
    partners = (
        [place.at(dx=i) for i in (1, 2, 3)]
        + [place.at(dy=i) for i in (1, 2, 3)]
        + [place.other_end(i) for i in range(NZL)]
        + col_peers
    )
    for device in partners:
        pl.semaphore_signal(barrier, inc=1, device_id=device, device_id_type=MESH)

    tok_rows = e.shape[0]
    step_rows = tok_rows // 2
    for first in range(0, tok_rows, step_rows):
        rotated = dot_nn(e[first : first + step_rows], rot[...])
        residue = rotated.T - rebuilt[:, first : first + step_rows]
        squares = residue * residue
        err[:, first : first + step_rows] = jnp.sum(squares.reshape(squares.shape[0] // 8, 8, step_rows), axis=0)
    pl.semaphore_wait(barrier, len(partners))

    total = jnp.sum(finish_sum(share_sum(place, sems, err, err_in, col_peers), err, err_in), axis=0, keepdims=True)
    weights = 1.0 / (1.0 + total / (2.0 * width))
    wt[...] = (rebuilt[...] * weights).astype(BF)

    block = out.shape[2]
    n_half = wt.shape[0] // 2
    x_cols = e.shape[1] // NX

    def chunk_a(xi):
        start = pl.multiple_of(xi * x_cols, x_cols)
        value = dot_nn(wt[0:n_half], e[:, pl.ds(start, x_cols)])
        for zh in range(NZH):
            for y in range(NY):
                at_in, at_out = (zh * NY + y) * block, (y * NZH + zh) * block
                keep_a[:, at_out : at_out + block] = value[:, at_in : at_in + block]

    def chunk_b(yi):
        parts = []
        for x in range(NX):
            for zh in range(NZH):
                start = pl.multiple_of(x * x_cols + (zh * NY + yi) * block, block)
                parts.append(e[:, pl.ds(start, block)])
        keep_b[...] = dot_nn(wt[n_half:], jnp.concatenate(parts, axis=1))

    def piece(source, keep):
        def chunk(i):
            width_of = keep.shape[1]
            keep[...] = source[:, pl.ds(pl.multiple_of(i * width_of, width_of), width_of)]

        return chunk

    run(
        ring_scatter(place, sems, "x", chunk_a, own_a, keep_a, *[big.at[0, i] for i in range(6)]),
        ring_scatter(place, sems, "y", chunk_b, own_b, keep_b, *[big.at[1, i] for i in range(6)]),
    )
    run(
        ring_scatter(place, sems, "y", piece(own_a, red.at[0]), ab.at[0], red.at[0], *[small.at[0, i] for i in range(6)]),
        ring_scatter(place, sems, "x", piece(own_b, red.at[1]), ab.at[1], red.at[1], *[small.at[1, i] for i in range(6)]),
    )
    ab_out[...] = ab[1 - place.zh].astype(BF)
    s = sems.take()
    swap = sems.copy(ab_out, ab_in, s, place.at(dz=4))
    swap.start()
    for zh in range(NZH):
        rows = pl.ds(pl.multiple_of(place.x * x_cols + (zh * NY + place.y) * block, block), block)
        cols = pl.ds(pl.multiple_of(place.zh * n_half, n_half), n_half)
        xo[:, zh * block : (zh + 1) * block] = prior_scale * rot[rows, cols].astype(F32).T
    swap.wait()
    x_new = ab[place.zh] + ab_in[...].astype(F32) + xo[...]
    xo[...] = x_new
    squares = x_new * x_new
    folded = jnp.sum(squares.reshape(squares.shape[0] // 8, 8, squares.shape[1]), axis=0)
    part = folded[:, 0:128]
    for i in range(1, folded.shape[1] // 128):
        part = part + folded[:, i * 128 : (i + 1) * 128]
    sq[0] = part

    y_copies = share_sum(place, sems, sq.at[0], sq_in.at[0], [place.at(dy=i) for i in (1, 2, 3)])
    inv = None
    for step in range(2):
        b_ref, a_ref, g_ref = bt.at[step], at.at[step], gfull.at[step]
        parts, rows = a_ref.shape[0], a_ref.shape[4]
        wide = NZH * NC * rows
        b_ref[place.y] = xo[...].astype(BF)
        panel = [ring_gather(place, sems, "y", b_ref, r * rows, rows) for r in range(parts)]
        for g in panel:
            next(g)
        spread = Spread(place, sems, b_ref, a_ref)

        def reduce_gram(r):
            total = None
            for q in range(NY):
                term = dot_nt(b_ref[q], a_ref[r, q].reshape(wide, a_ref.shape[5]))
                total = term if total is None else total + term
            gkeep[r] = total
            g_rows = total.shape[0] // NX

            def chunk_g(xi):
                gtake[r] = gkeep[r, pl.ds(pl.multiple_of(xi * g_rows, g_rows), g_rows)]

            yield from ring_scatter(
                place, sems, "x", chunk_g, gown.at[r], gtake.at[r], *[gbuf.at[step, r, i] for i in range(6)]
            )
            g_ref[r, place.x] = gown[r].astype(BF)
            yield from ring_gather(place, sems, "x", g_ref.at[r])

        grams = []
        done = 0
        for seg in range(parts + 1):
            need = parts if seg > 1 else seg + 1
            while done < min(need, parts):
                run(panel[done])
                done += 1
            spread.steps(seg * spread.slots, (seg + 1) * spread.slots)
            if seg > 0:
                if done < parts:
                    run(*panel[done:])
                    done = parts
                spread.arrived(seg - 1)
                pump(grams)
                g = reduce_gram(seg - 1)
                next(g)
                grams.append(g)
            if step == 0 and seg == 1:
                sq[1] = finish_sum(y_copies, sq.at[0], sq_in.at[0])
                z_copies = share_sum(place, sems, sq.at[1], sq_in.at[1], [place.at(dz=i) for i in range(1, 8)])
            if step == 0 and seg == 3:
                sq[2] = finish_sum(z_copies, sq.at[1], sq_in.at[1])
                c_copies = share_sum(place, sems, sq.at[2], sq_in.at[2], [place.at(dc=1)])
        if step == 0:
            sq[3] = finish_sum(c_copies, sq.at[2], sq_in.at[2])
            x_copies = share_sum(place, sems, sq.at[3], sq_in.at[3], [place.at(dx=i) for i in (1, 2, 3)])
        run(*grams)
        if step == 0:
            total = jnp.sum(finish_sum(x_copies, sq.at[3], sq_in.at[3]))
            scale2 = jnp.full((8, 128), 1.96 / width, F32) * total
            inv = 1.0 / jnp.sqrt(scale2)

        def chunk_y(q):
            value = None
            for r in range(parts):
                gram = jnp.concatenate([g_ref[r, i] for i in range(NX)], axis=0)
                term = dot_nn(gram, a_ref[r, q].reshape(wide, a_ref.shape[5]))
                value = term if value is None else value + term
            ykeep[...] = value

        run(ring_scatter(place, sems, "y", chunk_y, red.at[0], ykeep, *[ybuf.at[step, i] for i in range(6)]))
        if step == 0:
            f = jnp.tile(inv[0:1], (1, xo.shape[1] // 128))
            xo[...] = (1.5 * xo[...] - 0.5 * (red[0] * (f * f))) * f
        else:
            xo[...] = math.sqrt(width) * (1.5 * xo[...] - 0.5 * red[0])
        spread.sent()
    s = sems.take()
    mine = pl.ds(pl.multiple_of(place.zh * block, block), block)
    theirs = pl.ds(pl.multiple_of((1 - place.zh) * block, block), block)
    last_out[...] = xo[:, theirs].astype(last_out.dtype)
    swap = sems.copy(last_out, last_in, s, place.at(dz=4))
    swap.start()
    out[place.zh] = xo[:, mine]
    swap.wait()
    out[1 - place.zh] = last_in[...].astype(F32)


def shards(embeddings, rotation, codes, codebooks):
    tok_rows, width = embeddings.shape
    cols = rotation.shape[1]
    subs, centroids, sub_width = codebooks.shape
    rows_total = tok_rows * lax.axis_size("dp")
    block = width // lax.axis_size("dp")
    rebuilt = pl.pallas_call(
        rebuild_kernel,
        out_shape=jax.ShapeDtypeStruct((subs, sub_width, tok_rows), F32),
        in_specs=[pl.BlockSpec(memory_space=pltpu.VMEM)] * 2,
        out_specs=pl.BlockSpec(memory_space=pltpu.VMEM),
        name="rebuild",
    )(codes.T, codebooks.transpose(0, 2, 1)).reshape(cols, tok_rows)
    n = cols // NZH
    m = NZH * block
    panel = m * NY
    parts = 4
    rows = n // parts
    wide = NZH * NC * rows
    vm = pltpu.VMEM
    out_t = pl.pallas_call(
        functools.partial(main_kernel, 0.2 * rows_total, width),
        out_shape=jax.ShapeDtypeStruct((NZH, n, block), F32),
        in_specs=[pl.BlockSpec(memory_space=pltpu.VMEM)] * 3,
        out_specs=pl.BlockSpec(memory_space=pltpu.VMEM),
        scratch_shapes=[
            vm((cols, tok_rows), BF), vm((8, tok_rows), F32), vm((NZL * NC - 1, 8, tok_rows), F32),
            vm((n, panel), F32), vm((n, panel), F32),
            vm((2, 6, n, panel), BF), vm((2, 6, n, m), BF),
            vm((n, panel), F32), vm((n, panel), F32),
            vm((2, n, m), F32), vm((n, m), BF), vm((n, m), BF),
            vm((n, m), F32), vm((2, n, m), F32),
            vm((2, NY, n, m), BF), vm((2, parts, NY, NZH, NC, rows, m), BF),
            vm((parts, n, wide), F32), vm((parts, n // NX, wide), F32),
            vm((2, parts, 6, n // NX, wide), BF), vm((parts, n // NX, wide), F32),
            vm((2, parts, NX, n // NX, wide), BF),
            vm((n, m), F32), vm((2, 6, n, m), BF),
            vm((4, 8, 128), F32), vm((4, 7, 8, 128), F32),
            vm((n, block), BF), vm((n, block), BF),
            pltpu.SemaphoreType.DMA((NSEM,)), pltpu.SemaphoreType.DMA((NSEM,)),
        ],
        compiler_params=pltpu.CompilerParams(collective_id=0, has_side_effects=True, vmem_limit_bytes=60 * 2**20),
        name="main",
    )(rebuilt, embeddings, rotation)
    return out_t.reshape(cols, block).T


def solution(mesh):
    placed = (P("dp", None), P(None, "col"), P("dp", "col"), P("col", None, None))
    return jax.shard_map(
        shards, mesh=mesh, in_specs=placed, out_specs=P("dp", "col"), check_vma=False
    )
```

time: 243 us -> 261 us (1.074)
  Pallas kernels: 179 us -> 256 us
  local copies, waits for them, and re-layouts: 22.2 us -> 1.79 us
  blocking collectives: 17.7 us -> 0 us
  other arithmetic: 13.5 us -> 0 us
  matrix products: 9.13 us -> 0 us
    pallas_call x1, Pallas kernels: 179 us -> 252 us  [shards(): pl.pallas_call(functools.partial(main_kernel, 0.2 * rows_total, width), o...]
    psum x1 -> x0, blocking collectives: 17.7 us -> none  [shards(): row_error = lax.psum(jnp.sum(residue * residue, axis=1), 'col')]
    eq x4 -> x0, other arithmetic: 12.1 us -> none  [rebuild_rows(): sub_ids[:, :, None] == centroid_ids[None, None, :]]
    unnamed x18 -> x0, local copies, waits for them, and re-layouts: 10.9 us -> none
    dot_general x5 -> x0, matrix products: 9.13 us -> none  [the longest x4 6.74 us: rebuild_rows(): jnp.dot(onehot, block_table, preferred_element_type=jnp.float32)]
    reshape x1 -> x0, local copies, waits for them, and re-layouts: 6.91 us -> none  [shards(): panels = rotation.reshape(NX, NZH, NY, block, NZH, cols // NZH)]
    pallas_call x0 -> x1, Pallas kernels: none -> 3.9 us  [shards(): pl.pallas_call(rebuild_kernel, out_shape=jax.ShapeDtypeStruct((subs, sub_...]
where the time goes in v2:
time: 261 us; the launch traced here: 258 us
  Pallas kernels  256 us (98%)
    pallas_call x1, Pallas kernels, shards(): pl.pallas_call(functools.partial(main_kernel, 0.2 * rows_total, width), o...  252 us

profile of v2, /device:TPU:2, one launch (start us, length us, event | category | flops | bytes accessed | tf_op | source)
XLA Modules:
  0.0 258.1 jit_solution(14687762979285719705)
XLA Ops:
  0.0 3.9 %rebuild.1 = f32[64,8,512]{2,1,0:T(8,128)} custom-call(s32[64,512]{1,0:T(8,128)} %bitcast.8, bf16[64,8,256]{2,1,0:T(8,128)(2,1)} %bitcast.7), custom_call_target="tpu_custom_call" | custom-call | tf_op jit(solution)/shard_map/rebuild/pallas_call | solution.py:488
  3.9 252.4 %main.1 = f32[2,256,128]{2,1,0:T(8,128)} custom-call(f32[512,512]{1,0:T(8,128)} %bitcast.5, bf16[512,4096]{1,0:T(8,128)(2,1)} %e.1, bf16[4096,512]{1,0:T(8,128)(2,1)} %rot.1), custom_call_target="tpu_custom_call" | custom-call | tf_op jit(solution)/shard_map/main/pallas_call | solution.py:502
  256.3 1.8 copy.5

commit v3 on v2

--- a/solution.py
+++ b/solution.py
@@ -13,6 +13,9 @@
 F32 = jnp.float32
 NX, NY, NZH, NZL, NC = 4, 4, 2, 4, 2
 NSEM = 480
+LAG = 3
+PARTS = 4
+PAIR = 2
 
 
 def rebuild_kernel(codes, table, out):
@@ -183,7 +186,7 @@
         self.up, self.down, self.other = place.at(dz=1), place.at(dz=-1), place.at(dc=1)
         self.up_origin = ((z - self.d + 8) % 8) // 4
         self.down_origin = ((z + self.back) % 8) // 4
-        self.parts, self.slots = at.shape[0], at.shape[1]
+        self.parts, self.slots = at.shape[0], at.shape[1] // PAIR
         self.rows = at.shape[4]
         self.count = self.parts * self.slots
         n = self.count
@@ -192,15 +195,14 @@
         self.s_core = sems.take(2 * n)
 
     def spot(self, origin, n, part=None):
-        ref = self.at.at[n // self.slots, n % self.slots, origin, self.place.c]
+        blocks = pl.ds((n % self.slots) * PAIR, PAIR)
         half = self.rows // 2
-        if part is not None:
-            ref = ref.at[pl.ds(part * half, half)]
-        return ref
+        rows = pl.ds(0, self.rows) if part is None else pl.ds(part * half, half)
+        return self.at.at[n // self.slots, blocks, origin, self.place.c, rows]
 
     def source(self, n):
         first = pl.multiple_of((n // self.slots) * self.rows, self.rows)
-        return self.bt.at[n % self.slots, pl.ds(first, self.rows)]
+        return self.bt.at[pl.ds((n % self.slots) * PAIR, PAIR), pl.ds(first, self.rows)]
 
     def full(self, up, n, from_source=False):
         origin = self.up_origin if up else self.down_origin
@@ -217,7 +219,7 @@
         src = self.source(n) if from_source else self.spot(origin, n)
         return self.sems.copy(src, self.spot(origin, n), self.s_core + origin * self.count + n, self.other)
 
-    def steps(self, first, last):
+    def steps(self, first, last, after=None):
         d, n_all, far = self.d, self.count, 1 - self.place.zh
 
         def slot(t, carry):
@@ -229,7 +231,7 @@
 
             for up, lag, last_d in ((True, d, 3), (False, self.back, 1)):
                 origin = self.up_origin if up else self.down_origin
-                n = t - lag
+                n = t - LAG * lag
 
                 @pl.when((d > 0) & (n >= 0) & (n < n_all))
                 def _(up=up, n=n, last_d=last_d, origin=origin):
@@ -245,14 +247,16 @@
 
                     self.core(origin, n).start()
 
-            n = t - 4
-
-            @pl.when((d == 0) & (n >= 0))
+            n = t - LAG * 4
+
+            @pl.when((d == 0) & (n >= 0) & (n < n_all))
             def _():
                 self.half(True, n, far).wait_recv()
                 self.half(False, n, far).wait_recv()
                 self.core(far, n).start()
 
+            if after is not None:
+                after(t)
             return carry
 
         lax.fori_loop(first, last, slot, 0)
@@ -264,8 +268,8 @@
 
         @pl.when(self.d == 0)
         def _():
-            for q in range(self.slots):
-                rows = pl.ds(r * self.rows, self.rows)
+            for q in range(self.slots * PAIR):
+                rows = pl.ds(pl.multiple_of(r * self.rows, self.rows), self.rows)
                 self.at[r, q, self.place.zh, self.place.c] = self.bt[q, rows]
 
     def sent(self):
@@ -288,6 +292,93 @@
             return carry
 
         lax.fori_loop(0, self.count, one, 0)
+
+
+class GramReduce:
+    def __init__(self, place, sems, spread, keep, bufs, full):
+        self.place, self.sems, self.spread = place, sems, spread
+        self.keep, self.bufs, self.full = keep, bufs, full
+        self.s = sems.take(10 * full.shape[0])
+        self.right, self.left = place.at(dx=1), place.at(dx=-1)
+        self.rows = full.shape[2]
+        self.half = self.rows // 2
+        self.lo, self.hi = pl.ds(0, self.half), pl.ds(self.half, self.half)
+
+    def sc(self, r, i):
+        diag, got, to_r, to_l, from_l, from_r = [self.bufs.at[r, k] for k in range(6)]
+        src, dst, part, device = (
+            (diag, got, self.lo, self.right),
+            (diag, got, self.hi, self.left),
+            (to_r, from_l, self.hi, self.right),
+            (to_r, from_l, self.lo, self.right),
+            (to_l, from_r, self.lo, self.left),
+            (to_l, from_r, self.hi, self.left),
+        )[i]
+        return self.sems.copy(src.at[part], dst.at[part], self.s + 10 * r + i, device)
+
+    def ga(self, r, i):
+        x = self.place.x
+        slot, part, device = (
+            (x, pl.ds(0, self.rows), self.right),
+            (x, pl.ds(0, self.rows), self.left),
+            ((x + 3) % 4, self.lo, self.right),
+            ((x + 1) % 4, self.hi, self.left),
+        )[i]
+        ref = self.full.at[r, slot, part]
+        return self.sems.copy(ref, ref, self.s + 10 * r + 6 + i, device)
+
+    def mine(self, r, i, part):
+        first = i * self.rows + part * self.half
+        return self.keep[r, pl.ds(pl.multiple_of(first, self.half), self.half)]
+
+    def stage(self, number, r):
+        x = self.place.x
+        if number == 0:
+            self.spread.arrived(r)
+            bt, at = self.spread.bt, self.spread.at
+            wide = at.shape[2] * at.shape[3] * at.shape[4]
+            total = None
+            for q in range(at.shape[1]):
+                term = dot_nt(bt[q], at[r, q].reshape(wide, at.shape[5]))
+                total = term if total is None else total + term
+            self.keep[r] = total
+            for part, rows in ((0, self.lo), (1, self.hi)):
+                self.bufs[r, 0, rows] = self.mine(r, (x + 2) % 4, part).astype(BF)
+            self.sc(r, 0).start()
+            self.sc(r, 1).start()
+            self.bufs[r, 2, self.hi] = self.mine(r, (x + 1) % 4, 1).astype(BF)
+            self.sc(r, 2).start()
+            self.bufs[r, 3, self.lo] = self.mine(r, (x + 3) % 4, 0).astype(BF)
+            self.sc(r, 4).start()
+        elif number == 1:
+            self.sc(r, 0).wait_recv()
+            got = self.bufs[r, 1, self.lo].astype(F32)
+            self.bufs[r, 2, self.lo] = (self.mine(r, (x + 1) % 4, 0) + got).astype(BF)
+            self.sc(r, 3).start()
+            self.sc(r, 1).wait_recv()
+            got = self.bufs[r, 1, self.hi].astype(F32)
+            self.bufs[r, 3, self.hi] = (self.mine(r, (x + 3) % 4, 1) + got).astype(BF)
+            self.sc(r, 5).start()
+        elif number == 2:
+            for i in (2, 3, 4, 5):
+                self.sc(r, i).wait_recv()
+            for part, rows in ((0, self.lo), (1, self.hi)):
+                total = self.mine(r, x, part) + self.bufs[r, 4, rows].astype(F32) + self.bufs[r, 5, rows].astype(F32)
+                self.full[r, x, rows] = total.astype(BF)
+            self.ga(r, 0).start()
+            self.ga(r, 1).start()
+        elif number == 3:
+            self.ga(r, 0).wait_recv()
+            self.ga(r, 2).start()
+            self.ga(r, 1).wait_recv()
+            self.ga(r, 3).start()
+        else:
+            self.ga(r, 2).wait_recv()
+            self.ga(r, 3).wait_recv()
+            for i in range(6):
+                self.sc(r, i).wait_send()
+            for i in range(4):
+                self.ga(r, i).wait_send()
 
 
 def share_sum(place, sems, mine, slots, partners):
@@ -310,7 +401,7 @@
 def main_kernel(
     prior_scale, width, rebuilt, e, rot, out,
     wt, err, err_in, keep_a, keep_b, big, small, own_a, own_b, ab, ab_out, ab_in, xo, red,
-    bt, at, gkeep, gtake, gbuf, gown, gfull, ykeep, ybuf, sq, sq_in, last_out, last_in,
+    bt, at, gkeep, gbuf, gfull, ykeep, ybuf, sq, sq_in, last_out, last_in,
     send, recv,
 ):
     place = Place()
@@ -403,55 +494,32 @@
         for g in panel:
             next(g)
         spread = Spread(place, sems, b_ref, a_ref)
-
-        def reduce_gram(r):
-            total = None
-            for q in range(NY):
-                term = dot_nt(b_ref[q], a_ref[r, q].reshape(wide, a_ref.shape[5]))
-                total = term if total is None else total + term
-            gkeep[r] = total
-            g_rows = total.shape[0] // NX
-
-            def chunk_g(xi):
-                gtake[r] = gkeep[r, pl.ds(pl.multiple_of(xi * g_rows, g_rows), g_rows)]
-
-            yield from ring_scatter(
-                place, sems, "x", chunk_g, gown.at[r], gtake.at[r], *[gbuf.at[step, r, i] for i in range(6)]
-            )
-            g_ref[r, place.x] = gown[r].astype(BF)
-            yield from ring_gather(place, sems, "x", g_ref.at[r])
-
-        grams = []
-        done = 0
-        for seg in range(parts + 1):
-            need = parts if seg > 1 else seg + 1
-            while done < min(need, parts):
-                run(panel[done])
-                done += 1
-            spread.steps(seg * spread.slots, (seg + 1) * spread.slots)
-            if seg > 0:
-                if done < parts:
-                    run(*panel[done:])
-                    done = parts
-                spread.arrived(seg - 1)
-                pump(grams)
-                g = reduce_gram(seg - 1)
-                next(g)
-                grams.append(g)
-            if step == 0 and seg == 1:
-                sq[1] = finish_sum(y_copies, sq.at[0], sq_in.at[0])
-                z_copies = share_sum(place, sems, sq.at[1], sq_in.at[1], [place.at(dz=i) for i in range(1, 8)])
-            if step == 0 and seg == 3:
-                sq[2] = finish_sum(z_copies, sq.at[1], sq_in.at[1])
-                c_copies = share_sum(place, sems, sq.at[2], sq_in.at[2], [place.at(dc=1)])
+        grams = GramReduce(place, sems, spread, gkeep, gbuf.at[step], g_ref)
+        per, gap, stages = spread.slots, spread.slots, 5
+        d = spread.d
+        hops = 4 - d + (d // 3) * 2
+
+        def after(t):
+            for number in reversed(range(stages)):
+                ahead = t - gap * number - (per - 1) - LAG * hops
+
+                @pl.when((ahead >= 0) & (ahead % per == 0) & (ahead < per * parts))
+                def _(number=number, ahead=ahead):
+                    grams.stage(number, ahead // per)
+
+        run(panel[0])
+        for g in panel[1:]:
+            next(g)
+        for r in range(1, parts):
+            spread.steps((r - 1) * per, r * per)
+            run(panel[r])
         if step == 0:
-            sq[3] = finish_sum(c_copies, sq.at[2], sq_in.at[2])
-            x_copies = share_sum(place, sems, sq.at[3], sq_in.at[3], [place.at(dx=i) for i in (1, 2, 3)])
-        run(*grams)
+            sq[1] = finish_sum(y_copies, sq.at[0], sq_in.at[0])
+            z_copies = share_sum(place, sems, sq.at[1], sq_in.at[1], [place.at(dz=i) for i in range(1, 8)])
+        spread.steps((parts - 1) * per, parts * per + LAG * 4 + gap * (stages - 1), after)
         if step == 0:
-            total = jnp.sum(finish_sum(x_copies, sq.at[3], sq_in.at[3]))
-            scale2 = jnp.full((8, 128), 1.96 / width, F32) * total
-            inv = 1.0 / jnp.sqrt(scale2)
+            sq[2] = finish_sum(z_copies, sq.at[1], sq_in.at[1])
+            c_copies = share_sum(place, sems, sq.at[2], sq_in.at[2], [place.at(dc=1)])
 
         def chunk_y(q):
             value = None
@@ -461,7 +529,16 @@
                 value = term if value is None else value + term
             ykeep[...] = value
 
-        run(ring_scatter(place, sems, "y", chunk_y, red.at[0], ykeep, *[ybuf.at[step, i] for i in range(6)]))
+        product = [ring_scatter(place, sems, "y", chunk_y, red.at[0], ykeep, *[ybuf.at[step, i] for i in range(6)])]
+        pump(product)
+        if step == 0:
+            sq[3] = finish_sum(c_copies, sq.at[2], sq_in.at[2])
+            x_copies = share_sum(place, sems, sq.at[3], sq_in.at[3], [place.at(dx=i) for i in (1, 2, 3)])
+        run(*product)
+        if step == 0:
+            total = jnp.sum(finish_sum(x_copies, sq.at[3], sq_in.at[3]))
+            scale2 = jnp.full((8, 128), 1.96 / width, F32) * total
+            inv = 1.0 / jnp.sqrt(scale2)
         if step == 0:
             f = jnp.tile(inv[0:1], (1, xo.shape[1] // 128))
             xo[...] = (1.5 * xo[...] - 0.5 * (red[0] * (f * f))) * f
@@ -495,7 +572,7 @@
     n = cols // NZH
     m = NZH * block
     panel = m * NY
-    parts = 4
+    parts = PARTS
     rows = n // parts
     wide = NZH * NC * rows
     vm = pltpu.VMEM
@@ -512,8 +589,7 @@
             vm((2, n, m), F32), vm((n, m), BF), vm((n, m), BF),
             vm((n, m), F32), vm((2, n, m), F32),
             vm((2, NY, n, m), BF), vm((2, parts, NY, NZH, NC, rows, m), BF),
-            vm((parts, n, wide), F32), vm((parts, n // NX, wide), F32),
-            vm((2, parts, 6, n // NX, wide), BF), vm((parts, n // NX, wide), F32),
+            vm((parts, n, wide), F32), vm((2, parts, 6, n // NX, wide), BF),
             vm((2, parts, NX, n // NX, wide), BF),
             vm((n, m), F32), vm((2, 6, n, m), BF),
             vm((4, 8, 128), F32), vm((4, 7, 8, 128), F32),

time: 261 us -> 192 us (0.74)
  Pallas kernels: 256 us -> 190 us
    pallas_call x1, Pallas kernels: 252 us -> 186 us  [shards(): pl.pallas_call(functools.partial(main_kernel, 0.2 * rows_total, width), o...]
where the time goes in v3:
time: 192 us
  Pallas kernels  190 us (99%)
    pallas_call x1, Pallas kernels, shards(): pl.pallas_call(functools.partial(main_kernel, 0.2 * rows_total, width), o...  186 us
    pallas_call x1, Pallas kernels, shards(): pl.pallas_call(rebuild_kernel, out_shape=jax.ShapeDtypeStruct((subs, sub_...  3.9 us

profile of v3, /device:TPU:2, one launch (start us, length us, event | category | flops | bytes accessed | tf_op | source)
XLA Modules:
  0.0 191.7 jit_solution(10714998138719674945)
XLA Ops:
  0.0 3.9 %rebuild.1 = f32[64,8,512]{2,1,0:T(8,128)} custom-call(s32[64,512]{1,0:T(8,128)} %bitcast.8, bf16[64,8,256]{2,1,0:T(8,128)(2,1)} %bitcast.7), custom_call_target="tpu_custom_call" | custom-call | tf_op jit(solution)/shard_map/rebuild/pallas_call | solution.py:565
  3.9 186.0 %main.1 = f32[2,256,128]{2,1,0:T(8,128)} custom-call(f32[512,512]{1,0:T(8,128)} %bitcast.5, bf16[512,4096]{1,0:T(8,128)(2,1)} %e.1, bf16[4096,512]{1,0:T(8,128)(2,1)} %rot.1), custom_call_target="tpu_custom_call" | custom-call | tf_op jit(solution)/shard_map/main/pallas_call | solution.py:579
  189.9 1.8 copy.5

commit v4 on v3

--- a/solution.py
+++ b/solution.py
@@ -16,6 +16,8 @@
 LAG = 3
 PARTS = 4
 PAIR = 2
+GAP = 2
+SUB = 2
 
 
 def rebuild_kernel(codes, table, out):
@@ -99,42 +101,45 @@
         )
 
 
-def ring_scatter(place, sems, axis, chunk, out, keep, diag, got, to_r, to_l, from_l, from_r):
-    rows = diag.shape[0]
+def ring_scatter(place, sems, axis, value, emit, bufs, first, rows, prepare=None):
+    diag, got, to_r, to_l, from_l, from_r = bufs
     half = rows // 2
-    lo, hi = pl.ds(0, half), pl.ds(half, half)
+    lo, hi = pl.ds(first, half), pl.ds(first + half, half)
     p = place.index(axis)
     right, left = place.along(axis, 1), place.along(axis, -1)
     s = sems.take(6)
-    chunk((p + 2) % 4)
-    diag[...] = keep[...].astype(BF)
+    ready = prepare if prepare is not None else lambda i: None
+    ready((p + 2) % 4)
+    diag[lo] = value((p + 2) % 4, lo).astype(BF)
     c0 = sems.copy(diag.at[lo], got.at[lo], s, right)
+    c0.start()
+    diag[hi] = value((p + 2) % 4, hi).astype(BF)
     c1 = sems.copy(diag.at[hi], got.at[hi], s + 1, left)
-    c0.start()
     c1.start()
     yield
-    chunk((p + 1) % 4)
-    to_r[hi] = keep[hi].astype(BF)
+    ready((p + 1) % 4)
+    to_r[hi] = value((p + 1) % 4, hi).astype(BF)
     c2 = sems.copy(to_r.at[hi], from_l.at[hi], s + 2, right)
     c2.start()
+    ready((p + 3) % 4)
+    to_l[lo] = value((p + 3) % 4, lo).astype(BF)
+    c4 = sems.copy(to_l.at[lo], from_r.at[lo], s + 4, left)
+    c4.start()
+    yield
     c0.wait_recv()
-    to_r[lo] = (keep[lo] + got[lo].astype(F32)).astype(BF)
+    to_r[lo] = (value((p + 1) % 4, lo) + got[lo].astype(F32)).astype(BF)
     c3 = sems.copy(to_r.at[lo], from_l.at[lo], s + 3, right)
     c3.start()
-    yield
-    chunk((p + 3) % 4)
-    to_l[lo] = keep[lo].astype(BF)
-    c4 = sems.copy(to_l.at[lo], from_r.at[lo], s + 4, left)
-    c4.start()
     c1.wait_recv()
-    to_l[hi] = (keep[hi] + got[hi].astype(F32)).astype(BF)
+    to_l[hi] = (value((p + 3) % 4, hi) + got[hi].astype(F32)).astype(BF)
     c5 = sems.copy(to_l.at[hi], from_r.at[hi], s + 5, left)
     c5.start()
+    ready(p)
     yield
-    chunk(p)
     for c in (c2, c3, c4, c5):
         c.wait_recv()
-    out[...] = keep[...] + from_l[...].astype(F32) + from_r[...].astype(F32)
+    for part in (lo, hi):
+        emit(part, value(p, part) + from_l[part].astype(F32) + from_r[part].astype(F32))
     for c in (c0, c1, c2, c3, c4, c5):
         c.wait_send()
 
@@ -400,8 +405,8 @@
 
 def main_kernel(
     prior_scale, width, rebuilt, e, rot, out,
-    wt, err, err_in, keep_a, keep_b, big, small, own_a, own_b, ab, ab_out, ab_in, xo, red,
-    bt, at, gkeep, gbuf, gfull, ykeep, ybuf, sq, sq_in, last_out, last_in,
+    wt, err, err_in, part_a, part_b, big, small, own_a, own_b, ab, ab_out, ab_in, xo, red,
+    bt, at, gkeep, gbuf, gfull, yk, ybuf, sq, sq_in, last_out, last_in,
     send, recv,
 ):
     place = Place()
@@ -434,49 +439,91 @@
     n_half = wt.shape[0] // 2
     x_cols = e.shape[1] // NX
 
-    def chunk_a(xi):
+    def compute_a(xi):
         start = pl.multiple_of(xi * x_cols, x_cols)
         value = dot_nn(wt[0:n_half], e[:, pl.ds(start, x_cols)])
         for zh in range(NZH):
             for y in range(NY):
                 at_in, at_out = (zh * NY + y) * block, (y * NZH + zh) * block
-                keep_a[:, at_out : at_out + block] = value[:, at_in : at_in + block]
-
-    def chunk_b(yi):
+                part_a[xi, :, at_out : at_out + block] = value[:, at_in : at_in + block]
+
+    def compute_b(yi):
         parts = []
         for x in range(NX):
             for zh in range(NZH):
                 start = pl.multiple_of(x * x_cols + (zh * NY + yi) * block, block)
                 parts.append(e[:, pl.ds(start, block)])
-        keep_b[...] = dot_nn(wt[n_half:], jnp.concatenate(parts, axis=1))
-
-    def piece(source, keep):
-        def chunk(i):
-            width_of = keep.shape[1]
-            keep[...] = source[:, pl.ds(pl.multiple_of(i * width_of, width_of), width_of)]
-
-        return chunk
-
-    run(
-        ring_scatter(place, sems, "x", chunk_a, own_a, keep_a, *[big.at[0, i] for i in range(6)]),
-        ring_scatter(place, sems, "y", chunk_b, own_b, keep_b, *[big.at[1, i] for i in range(6)]),
-    )
-    run(
-        ring_scatter(place, sems, "y", piece(own_a, red.at[0]), ab.at[0], red.at[0], *[small.at[0, i] for i in range(6)]),
-        ring_scatter(place, sems, "x", piece(own_b, red.at[1]), ab.at[1], red.at[1], *[small.at[1, i] for i in range(6)]),
-    )
-    ab_out[...] = ab[1 - place.zh].astype(BF)
-    s = sems.take()
-    swap = sems.copy(ab_out, ab_in, s, place.at(dz=4))
-    swap.start()
+        part_b[yi] = dot_nn(wt[n_half:], jnp.concatenate(parts, axis=1))
+
+    sub = n_half // SUB
+    m = ab.shape[2]
+
+    def chain(which, k):
+        first_axis, second_axis = ("x", "y") if which == 0 else ("y", "x")
+        source, own = (part_a, own_a) if which == 0 else (part_b, own_b)
+        prepare = (compute_a if which == 0 else compute_b) if k == 0 else None
+
+        def keep_own(rows, total):
+            own[rows] = total
+
+        def keep_ab(rows, total):
+            ab[which, rows] = total
+
+        yield from ring_scatter(
+            place, sems, first_axis, lambda i, rows: source[i, rows], keep_own,
+            [big.at[which, i] for i in range(6)], k * sub, sub, prepare,
+        )
+        yield from ring_scatter(
+            place, sems, second_axis, lambda i, rows: own[rows, pl.ds(pl.multiple_of(i * m, m), m)], keep_ab,
+            [small.at[which, i] for i in range(6)], k * sub, sub,
+        )
+
+    def in_rounds(groups, finished, between=None):
+        groups = dict(enumerate(groups))
+        count = 0
+        while groups:
+            if between is not None:
+                between(count)
+            count += 1
+            for k in list(groups):
+                pump(groups[k])
+                if not groups[k]:
+                    del groups[k]
+                    finished(k)
+
+    swaps = []
+
+    def start_swap(k):
+        rows = pl.ds(k * sub, sub)
+        ab_out[rows] = ab[1 - place.zh, rows].astype(BF)
+        swap = sems.copy(ab_out.at[rows], ab_in.at[rows], sems.take(), place.at(dz=4))
+        swap.start()
+        swaps.append(swap)
+
     for zh in range(NZH):
         rows = pl.ds(pl.multiple_of(place.x * x_cols + (zh * NY + place.y) * block, block), block)
         cols = pl.ds(pl.multiple_of(place.zh * n_half, n_half), n_half)
         xo[:, zh * block : (zh + 1) * block] = prior_scale * rot[rows, cols].astype(F32).T
-    swap.wait()
-    x_new = ab[place.zh] + ab_in[...].astype(F32) + xo[...]
-    xo[...] = x_new
-    squares = x_new * x_new
+    in_rounds([[chain(0, k), chain(1, k)] for k in range(SUB)], start_swap)
+
+    parts, rows_r = at.shape[1], at.shape[5]
+    wide = NZH * NC * rows_r
+    panels = {0: [], 1: []}
+
+    def share_rows(step, k):
+        rows = pl.ds(k * sub, sub)
+        bt[step, place.y, rows] = xo[rows].astype(BF)
+        for r in range(k * parts // SUB, (k + 1) * parts // SUB):
+            g = ring_gather(place, sems, "y", bt.at[step], r * rows_r, rows_r)
+            next(g)
+            panels[step].append(g)
+
+    for k in range(SUB):
+        rows = pl.ds(k * sub, sub)
+        swaps[k].wait()
+        xo[rows] = ab[place.zh, rows] + ab_in[rows].astype(F32) + xo[rows]
+        share_rows(0, k)
+    squares = xo[...] * xo[...]
     folded = jnp.sum(squares.reshape(squares.shape[0] // 8, 8, squares.shape[1]), axis=0)
     part = folded[:, 0:128]
     for i in range(1, folded.shape[1] // 128):
@@ -484,18 +531,17 @@
     sq[0] = part
 
     y_copies = share_sum(place, sems, sq.at[0], sq_in.at[0], [place.at(dy=i) for i in (1, 2, 3)])
-    inv = None
+    mine = pl.ds(pl.multiple_of(place.zh * block, block), block)
+    theirs = pl.ds(pl.multiple_of((1 - place.zh) * block, block), block)
+    last = []
+    spreads = []
     for step in range(2):
         b_ref, a_ref, g_ref = bt.at[step], at.at[step], gfull.at[step]
-        parts, rows = a_ref.shape[0], a_ref.shape[4]
-        wide = NZH * NC * rows
-        b_ref[place.y] = xo[...].astype(BF)
-        panel = [ring_gather(place, sems, "y", b_ref, r * rows, rows) for r in range(parts)]
-        for g in panel:
-            next(g)
+        panel = panels[step]
         spread = Spread(place, sems, b_ref, a_ref)
+        spreads.append(spread)
         grams = GramReduce(place, sems, spread, gkeep, gbuf.at[step], g_ref)
-        per, gap, stages = spread.slots, spread.slots, 5
+        per, gap, stages = spread.slots, spread.slots * GAP, 5
         d = spread.d
         hops = 4 - d + (d // 3) * 2
 
@@ -521,39 +567,60 @@
             sq[2] = finish_sum(z_copies, sq.at[1], sq_in.at[1])
             c_copies = share_sum(place, sems, sq.at[2], sq_in.at[2], [place.at(dc=1)])
 
-        def chunk_y(q):
+        def compute_y(q):
             value = None
             for r in range(parts):
                 gram = jnp.concatenate([g_ref[r, i] for i in range(NX)], axis=0)
                 term = dot_nn(gram, a_ref[r, q].reshape(wide, a_ref.shape[5]))
                 value = term if value is None else value + term
-            ykeep[...] = value
-
-        product = [ring_scatter(place, sems, "y", chunk_y, red.at[0], ykeep, *[ybuf.at[step, i] for i in range(6)])]
-        pump(product)
-        if step == 0:
-            sq[3] = finish_sum(c_copies, sq.at[2], sq_in.at[2])
-            x_copies = share_sum(place, sems, sq.at[3], sq_in.at[3], [place.at(dx=i) for i in (1, 2, 3)])
-        run(*product)
-        if step == 0:
-            total = jnp.sum(finish_sum(x_copies, sq.at[3], sq_in.at[3]))
-            scale2 = jnp.full((8, 128), 1.96 / width, F32) * total
-            inv = 1.0 / jnp.sqrt(scale2)
-        if step == 0:
-            f = jnp.tile(inv[0:1], (1, xo.shape[1] // 128))
-            xo[...] = (1.5 * xo[...] - 0.5 * (red[0] * (f * f))) * f
-        else:
-            xo[...] = math.sqrt(width) * (1.5 * xo[...] - 0.5 * red[0])
+            yk[q] = value
+
+        def keep_y(rows, total):
+            red[rows] = total
+
+        def sums(count, step=step):
+            if step == 0 and count == 1:
+                sq[3] = finish_sum(shared["c"], sq.at[2], sq_in.at[2])
+                shared["x"] = share_sum(place, sems, sq.at[3], sq_in.at[3], [place.at(dx=i) for i in (1, 2, 3)])
+            if step == 0 and count == 3:
+                total = jnp.sum(finish_sum(shared["x"], sq.at[3], sq_in.at[3]))
+                scale2 = jnp.full((8, 128), 1.96 / width, F32) * total
+                shared["inv"] = jnp.tile((1.0 / jnp.sqrt(scale2))[0:1], (1, m // 128))
+
+        def finish_rows(k, step=step):
+            rows = pl.ds(k * sub, sub)
+            if step == 0:
+                f = shared["inv"]
+                xo[rows] = (1.5 * xo[rows] - 0.5 * (red[rows] * (f * f))) * f
+                share_rows(1, k)
+            else:
+                xo[rows] = math.sqrt(width) * (1.5 * xo[rows] - 0.5 * red[rows])
+                last_out[rows] = xo[rows, theirs].astype(BF)
+                swap = sems.copy(last_out.at[rows], last_in.at[rows], sems.take(), place.at(dz=4))
+                swap.start()
+                last.append(swap)
+                out[place.zh, rows] = xo[rows, mine]
+
+        shared = {"c": c_copies if step == 0 else None}
+        in_rounds(
+            [
+                [
+                    ring_scatter(
+                        place, sems, "y", lambda i, rows: yk[i, rows], keep_y,
+                        [ybuf.at[step, i] for i in range(6)], k * sub, sub, compute_y if k == 0 else None,
+                    )
+                ]
+                for k in range(SUB)
+            ],
+            finish_rows,
+            sums,
+        )
+    for spread in spreads:
         spread.sent()
-    s = sems.take()
-    mine = pl.ds(pl.multiple_of(place.zh * block, block), block)
-    theirs = pl.ds(pl.multiple_of((1 - place.zh) * block, block), block)
-    last_out[...] = xo[:, theirs].astype(last_out.dtype)
-    swap = sems.copy(last_out, last_in, s, place.at(dz=4))
-    swap.start()
-    out[place.zh] = xo[:, mine]
-    swap.wait()
-    out[1 - place.zh] = last_in[...].astype(F32)
+    for k in range(SUB):
+        rows = pl.ds(k * sub, sub)
+        last[k].wait()
+        out[1 - place.zh, rows] = last_in[rows].astype(F32)
 
 
 def shards(embeddings, rotation, codes, codebooks):
@@ -583,15 +650,15 @@
         out_specs=pl.BlockSpec(memory_space=pltpu.VMEM),
         scratch_shapes=[
             vm((cols, tok_rows), BF), vm((8, tok_rows), F32), vm((NZL * NC - 1, 8, tok_rows), F32),
-            vm((n, panel), F32), vm((n, panel), F32),
+            vm((NX, n, panel), F32), vm((NY, n, panel), F32),
             vm((2, 6, n, panel), BF), vm((2, 6, n, m), BF),
             vm((n, panel), F32), vm((n, panel), F32),
             vm((2, n, m), F32), vm((n, m), BF), vm((n, m), BF),
-            vm((n, m), F32), vm((2, n, m), F32),
+            vm((n, m), F32), vm((n, m), F32),
             vm((2, NY, n, m), BF), vm((2, parts, NY, NZH, NC, rows, m), BF),
             vm((parts, n, wide), F32), vm((2, parts, 6, n // NX, wide), BF),
             vm((2, parts, NX, n // NX, wide), BF),
-            vm((n, m), F32), vm((2, 6, n, m), BF),
+            vm((NY, n, m), F32), vm((2, 6, n, m), BF),
             vm((4, 8, 128), F32), vm((4, 7, 8, 128), F32),
             vm((n, block), BF), vm((n, block), BF),
             pltpu.SemaphoreType.DMA((NSEM,)), pltpu.SemaphoreType.DMA((NSEM,)),

time: 192 us -> 177 us (0.922)
  Pallas kernels: 190 us -> 175 us
    pallas_call x1, Pallas kernels: 186 us -> 171 us  [shards(): pl.pallas_call(functools.partial(main_kernel, 0.2 * rows_total, width), o...]
where the time goes in v4:
time: 177 us
  Pallas kernels  175 us (99%)
  local copies, waits for them, and re-layouts  1.79 us (1%)
    pallas_call x1, Pallas kernels, shards(): pl.pallas_call(functools.partial(main_kernel, 0.2 * rows_total, width), o...  171 us
    pallas_call x1, Pallas kernels, shards(): pl.pallas_call(rebuild_kernel, out_shape=jax.ShapeDtypeStruct((subs, sub_...  3.9 us

profile of v4, /device:TPU:2, one launch (start us, length us, event | category | flops | bytes accessed | tf_op | source)
XLA Modules:
  0.0 176.7 jit_solution(7721400905664480956)
XLA Ops:
  0.0 3.9 %rebuild.1 = f32[64,8,512]{2,1,0:T(8,128)} custom-call(s32[64,512]{1,0:T(8,128)} %bitcast.8, bf16[64,8,256]{2,1,0:T(8,128)(2,1)} %bitcast.7), custom_call_target="tpu_custom_call" | custom-call | tf_op jit(solution)/shard_map/rebuild/pallas_call | solution.py:632
  3.9 171.0 %main.1 = f32[2,256,128]{2,1,0:T(8,128)} custom-call(f32[512,512]{1,0:T(8,128)} %bitcast.5, bf16[512,4096]{1,0:T(8,128)(2,1)} %e.1, bf16[4096,512]{1,0:T(8,128)(2,1)} %rot.1), custom_call_target="tpu_custom_call" | custom-call | tf_op jit(solution)/shard_map/main/pallas_call | solution.py:646
  174.9 1.8 %copy.5 = f32[512,128]{0,1:T(8,128)} copy(f32[512,128]{1,0:T(8,128)} %bitcast.6) | data formatting | bytes 524288 | tf_op jit(solution)/shard_map/reshape | solution.py:669

commit v5 on v4

--- a/solution.py
+++ b/solution.py
@@ -12,12 +12,12 @@
 BF = jnp.bfloat16
 F32 = jnp.float32
 NX, NY, NZH, NZL, NC = 4, 4, 2, 4, 2
-NSEM = 480
+NSEM = 560
 LAG = 3
 PARTS = 4
 PAIR = 2
-GAP = 2
-SUB = 2
+GAP = 3
+SUB = 4
 
 
 def rebuild_kernel(codes, table, out):
@@ -38,7 +38,7 @@
             out[m, :, first : first + lanes] = value
         return carry
 
-    lax.fori_loop(0, codes.shape[0], one_subspace, 0, unroll=4)
+    lax.fori_loop(0, codes.shape[0], one_subspace, 0, unroll=8)
 
 
 def dot_nt(a, b):
@@ -404,11 +404,19 @@
 
 
 def main_kernel(
-    prior_scale, width, rebuilt, e, rot, out,
-    wt, err, err_in, part_a, part_b, big, small, own_a, own_b, ab, ab_out, ab_in, xo, red,
+    prior_scale, width, rebuilt, e_far, rot_far, out,
+    e, rot, near, wt, err, err_in, part_a, part_b, big, small, own_a, own_b, ab, ab_out, ab_in, xo, red,
     bt, at, gkeep, gbuf, gfull, yk, ybuf, sq, sq_in, last_out, last_in,
     send, recv,
 ):
+    tok_rows = e.shape[0]
+    step_rows = tok_rows // 2
+    staged = [pltpu.make_async_copy(rot_far, rot, near.at[0])]
+    for i in range(2):
+        rows = pl.ds(i * step_rows, step_rows)
+        staged.append(pltpu.make_async_copy(e_far.at[rows], e.at[rows], near.at[1 + i]))
+    for copy in staged:
+        copy.start()
     place = Place()
     sems = Sems(send, recv)
     barrier = pltpu.get_barrier_semaphore()
@@ -422,9 +430,9 @@
     for device in partners:
         pl.semaphore_signal(barrier, inc=1, device_id=device, device_id_type=MESH)
 
-    tok_rows = e.shape[0]
-    step_rows = tok_rows // 2
+    staged[0].wait()
     for first in range(0, tok_rows, step_rows):
+        staged[1 + first // step_rows].wait()
         rotated = dot_nn(e[first : first + step_rows], rot[...])
         residue = rotated.T - rebuilt[:, first : first + step_rows]
         squares = residue * residue
@@ -646,9 +654,10 @@
     out_t = pl.pallas_call(
         functools.partial(main_kernel, 0.2 * rows_total, width),
         out_shape=jax.ShapeDtypeStruct((NZH, n, block), F32),
-        in_specs=[pl.BlockSpec(memory_space=pltpu.VMEM)] * 3,
+        in_specs=[pl.BlockSpec(memory_space=pltpu.VMEM)] + [pl.BlockSpec(memory_space=pl.ANY)] * 2,
         out_specs=pl.BlockSpec(memory_space=pltpu.VMEM),
         scratch_shapes=[
+            vm((tok_rows, width), BF), vm((width, cols), BF), pltpu.SemaphoreType.DMA((3,)),
             vm((cols, tok_rows), BF), vm((8, tok_rows), F32), vm((NZL * NC - 1, 8, tok_rows), F32),
             vm((NX, n, panel), F32), vm((NY, n, panel), F32),
             vm((2, 6, n, panel), BF), vm((2, 6, n, m), BF),

time: 177 us -> 175 us (0.989)
  Pallas kernels: 175 us -> 173 us
where the time goes in v5:
time: 175 us
  Pallas kernels  173 us (99%)
  local copies, waits for them, and re-layouts  1.79 us (1%)
    pallas_call x1, Pallas kernels, shards(): pl.pallas_call(functools.partial(main_kernel, 0.2 * rows_total, width), o...  170 us

profile of v5, /device:TPU:2, one launch (start us, length us, event | category | flops | bytes accessed | tf_op | source)
XLA Modules:
  0.0 175.2 jit_solution(5382220959227097573)
XLA Ops:
  0.0 3.3 %rebuild.1 = f32[64,8,512]{2,1,0:T(8,128)} custom-call(s32[64,512]{1,0:T(8,128)} %bitcast.8, bf16[64,8,256]{2,1,0:T(8,128)(2,1)} %bitcast.7), custom_call_target="tpu_custom_call" | custom-call | tf_op jit(solution)/shard_map/rebuild/pallas_call | solution.py:640
  3.3 170.0 %main.1 = f32[2,256,128]{2,1,0:T(8,128)} custom-call(f32[512,512]{1,0:T(8,128)} %bitcast.5, bf16[512,4096]{1,0:T(8,128)(2,1)} %e_far.1, bf16[4096,512]{1,0:T(8,128)(2,1)} %rot_far.1), custom_call_target="tpu_custom_call" | custom-call | tf_op jit(solution)/shard_map/main/pallas_call | solution.py:654
  173.4 1.8 %copy.5 = f32[512,128]{0,1:T(8,128)} copy(f32[512,128]{1,0:T(8,128)} %bitcast.6) | data formatting | bytes 524288 | tf_op jit(solution)/shard_map/reshape | solution.py:678

commit v6 on v5

--- a/solution.py
+++ b/solution.py
@@ -28,7 +28,7 @@
         ids = codes[pl.ds(m, 1), :]
         for first in range(0, codes.shape[1], lanes):
             index = jnp.broadcast_to(ids[:, first : first + lanes], (entries.shape[0], lanes))
-            within = index % lanes
+            within = index & (lanes - 1)
             value = None
             for part in range(entries.shape[1] // lanes):
                 picked = jnp.take_along_axis(
@@ -436,10 +436,10 @@
         rotated = dot_nn(e[first : first + step_rows], rot[...])
         residue = rotated.T - rebuilt[:, first : first + step_rows]
         squares = residue * residue
-        err[:, first : first + step_rows] = jnp.sum(squares.reshape(squares.shape[0] // 8, 8, step_rows), axis=0)
+        err[:, first : first + step_rows] = jnp.sum(squares, axis=0, keepdims=True)
     pl.semaphore_wait(barrier, len(partners))
 
-    total = jnp.sum(finish_sum(share_sum(place, sems, err, err_in, col_peers), err, err_in), axis=0, keepdims=True)
+    total = finish_sum(share_sum(place, sems, err, err_in, col_peers), err, err_in)
     weights = 1.0 / (1.0 + total / (2.0 * width))
     wt[...] = (rebuilt[...] * weights).astype(BF)
 
@@ -508,11 +508,14 @@
         swap.start()
         swaps.append(swap)
 
-    for zh in range(NZH):
-        rows = pl.ds(pl.multiple_of(place.x * x_cols + (zh * NY + place.y) * block, block), block)
-        cols = pl.ds(pl.multiple_of(place.zh * n_half, n_half), n_half)
-        xo[:, zh * block : (zh + 1) * block] = prior_scale * rot[rows, cols].astype(F32).T
-    in_rounds([[chain(0, k), chain(1, k)] for k in range(SUB)], start_swap)
+    def add_prior(count):
+        if count == 2:
+            for zh in range(NZH):
+                rows = pl.ds(pl.multiple_of(place.x * x_cols + (zh * NY + place.y) * block, block), block)
+                cols = pl.ds(pl.multiple_of(place.zh * n_half, n_half), n_half)
+                xo[:, zh * block : (zh + 1) * block] = prior_scale * rot[rows, cols].astype(F32).T
+
+    in_rounds([[chain(0, k), chain(1, k)] for k in range(SUB)], start_swap, add_prior)
 
     parts, rows_r = at.shape[1], at.shape[5]
     wide = NZH * NC * rows_r
@@ -658,7 +661,7 @@
         out_specs=pl.BlockSpec(memory_space=pltpu.VMEM),
         scratch_shapes=[
             vm((tok_rows, width), BF), vm((width, cols), BF), pltpu.SemaphoreType.DMA((3,)),
-            vm((cols, tok_rows), BF), vm((8, tok_rows), F32), vm((NZL * NC - 1, 8, tok_rows), F32),
+            vm((cols, tok_rows), BF), vm((1, tok_rows), F32), vm((NZL * NC - 1, 1, tok_rows), F32),
             vm((NX, n, panel), F32), vm((NY, n, panel), F32),
             vm((2, 6, n, panel), BF), vm((2, 6, n, m), BF),
             vm((n, panel), F32), vm((n, panel), F32),

time: 175 us -> 175 us (level)
  no operation moved by 1% of the time
where the time goes in v6:
time: 175 us
  Pallas kernels  173 us (99%)
  local copies, waits for them, and re-layouts  1.79 us (1%)
    pallas_call x1, Pallas kernels, shards(): pl.pallas_call(functools.partial(main_kernel, 0.2 * rows_total, width), o...  170 us

profile of v6, /device:TPU:2, one launch (start us, length us, event | category | flops | bytes accessed | tf_op | source)
XLA Modules:
  0.0 174.8 jit_solution(7947078818315750202)
XLA Ops:
  0.0 3.3 %rebuild.1 = f32[64,8,512]{2,1,0:T(8,128)} custom-call(s32[64,512]{1,0:T(8,128)} %bitcast.8, bf16[64,8,256]{2,1,0:T(8,128)(2,1)} %bitcast.7), custom_call_target="tpu_custom_call" | custom-call | tf_op jit(solution)/shard_map/rebuild/pallas_call | solution.py:643
  3.3 169.7 %main.1 = f32[2,256,128]{2,1,0:T(8,128)} custom-call(f32[512,512]{1,0:T(8,128)} %bitcast.5, bf16[512,4096]{1,0:T(8,128)(2,1)} %e_far.1, bf16[4096,512]{1,0:T(8,128)(2,1)} %rot_far.1), custom_call_target="tpu_custom_call" | custom-call | tf_op jit(solution)/shard_map/main/pallas_call | solution.py:657
  173.0 1.8 %copy.5 = f32[512,128]{0,1:T(8,128)} copy(f32[512,128]{1,0:T(8,128)} %bitcast.6) | data formatting | bytes 524288 | tf_op jit(solution)/shard_map/reshape | solution.py:681
